TPU v7x, 32 devices: a whole 2x2x4 slice. The times are simulated.
32 devices in a mesh: tm: 32 (over z, y, x, core).
Axes of the slice: x: 2, y: 2, z: 4, core: 2. Of those that a mesh axis runs over, the one named last changes fastest.
Arguments:
- schur_inverse: float32 [32, 320, 320], P('tm'), as said below
- sweep_factor: float32 [32, 320, 320], P('tm')
Outputs:
- diagonal_blocks: float32 [32, 320, 320], P('tm')
- coupling_blocks: float32 [32, 320, 320], P('tm')
Inputs may be any that keep to these rules, and one draw needn't show every extreme that they name: Every block of schur_inverse is symmetric.
All inputs are finite; a program needn't handle non-finite values.
Results may differ from a plain program's by a relative error of at most 0.0003.
Values sent between devices are 32-bit elements; how exact they have to be, the bound alone decides.
A program may use at most 192 MiB of HBM per device.

v0:
```python
import functools

import jax
import jax.numpy as jnp
from jax import lax
from jax.experimental import pallas as pl
from jax.experimental.pallas import tpu as pltpu
from jax.sharding import PartitionSpec as P

MESH = pl.DeviceIdType.MESH
STRIP = 128
GROUP_LEVELS = 3
NN = (((1,), (0,)), ((), ()))
NT = (((1,), (1,)), ((), ()))


def dot(left, right, dims):
    return lax.dot_general(left, right, dims, preferred_element_type=jnp.float32)


def split(value, high, low):
    top = value.astype(jnp.bfloat16)
    high[...] = top
    low[...] = (value - top.astype(jnp.float32)).astype(jnp.bfloat16)


def product(left, right, dims):
    lh, ll = left
    rh, rl = right
    return (
        dot(lh[...], rl[...], dims) + dot(ll[...], rh[...], dims)
    ) + dot(lh[...], rh[...], dims)


def strips_of(order):
    return [(a, min(a + STRIP, order)) for a in range(0, order, STRIP)]


def kernel(n, levels, g_any, l_any, x_ref, q_ref, *scratch):
    (g_ref, l_ref, ro, rp, so, sp, to, tp, rx, prev, xt, xc, ph, pll, vh, vl, wh, wl,
     o_send, o_recv, p_send, p_recv, x_send, x_recv, n_send, n_recv, in_sem) = scratch
    order = g_ref.shape[0]
    strips = strips_of(order)
    count = len(strips)
    me = lax.axis_index("tm")
    size = 1 << levels
    j = lax.rem(me, size)
    group = me // size
    top = n // size - 1
    bits = [lax.rem(j // (1 << b), 2) for b in range(levels)]
    reach = [1 << b for b in range(levels)] + [size]
    even = bits[0] == 0
    odd = bits[0] == 1
    rest = group < top
    g_in = pltpu.make_async_copy(g_any, g_ref, in_sem.at[0])
    l_in = pltpu.make_async_copy(l_any, l_ref, in_sem.at[1])
    g_in.start()
    l_in.start()

    barrier = pltpu.get_barrier_semaphore()
    total = 0
    for d in reach:
        for other, inside in ((me + d, me + d < n), (me - d, me - d >= 0)):
            total = total + inside.astype(jnp.int32)

            @pl.when(inside)
            def _(other=other):
                pl.semaphore_signal(barrier, inc=1, device_id=(other,), device_id_type=MESH)

    g_in.wait()
    l_in.wait()
    pl.semaphore_wait(barrier, total)

    def copy(src, dst, send, recv, target):
        return pltpu.make_async_remote_copy(
            src_ref=src, dst_ref=dst, send_sem=send, recv_sem=recv,
            device_id=(target,), device_id_type=MESH,
        )

    pending = []

    def send(condition, make):
        @pl.when(condition)
        def _():
            make().start()
        pending.append((condition, make))

    wide = 2 * STRIP
    tail = order - wide

    def upper(ref, s):
        a, b = strips[s]
        return ref.at[a:b, :wide] if s < 2 else ref.at[a:b, wide:]

    def whole(ref, s):
        a, b = strips[s]
        return ref.at[a:b, :]

    def wanted(k):
        final = group == top
        for b in range(k + 1, levels):
            final = final & (bits[b] == 1)
        return jnp.logical_not(final)

    def put(value, rows, columns):
        split(value, vh.at[rows, columns], vl.at[rows, columns])

    first, second, third = slice(0, STRIP), slice(STRIP, wide), slice(wide, order)

    def split_strip(ref, s):
        if s == 0:
            put(ref[first, :wide], first, slice(0, wide))
            put(ref[first, second].T, second, first)
        elif s == 1:
            put(ref[second, second], second, second)
            tails = ref[second, first]
            turned = tails.T
            put(tails[:, :tail], first, third)
            put(tails[:, tail:2 * tail], second, third)
            put(turned[:tail], third, first)
            put(turned[tail:2 * tail], third, second)
        else:
            put(ref[third, third], third, third)

    def fold_strip(o_in, out, s):
        a, b = strips[s]
        rows = (ph.at[a:b, :], pll.at[a:b, :])
        split(product(rows, (vh, vl), NN), wh.at[a:b, :], wl.at[a:b, :])
        term = product((wh.at[a:b, :], wl.at[a:b, :]), (ph.at[a:, :], pll.at[a:, :]), NT)

        def store(rows, columns, value):
            out[rows, columns] = value if o_in is None else o_in[rows, columns] + value

        if s == 0:
            store(first, slice(0, wide), term[:, :wide])
            store(second, slice(0, tail), term[:, wide:])
        elif s == 1:
            store(second, second, term[:, :STRIP])
            store(second, slice(tail, 2 * tail), term[:, STRIP:])
        else:
            store(third, third, term)

    def factor_strip(out, s):
        a, b = strips[s]
        out[a:b, :] = product((ph.at[a:b, :], pll.at[a:b, :]), (vh, vl), NN)

    def partner(k):
        return jnp.where(bits[k] == 0, me + (1 << k), me - (1 << k))

    def arrive(ref, send_sem, recv_sem):
        copy(ref, ref, send_sem, recv_sem, me).wait_recv()

    def arrive_factor(k):
        for s in range(count):
            arrive(whole(rp.at[k], s), p_send.at[k, 0, s], p_recv.at[k, s])

    def arrive_offset(k, s):
        arrive(upper(ro.at[k], s), o_send.at[k, 0, s], o_recv.at[k, s])

    def send_factor(k, s, src, condition):
        send(
            even & condition & ((bits[k] == 0) | wanted(k)),
            lambda: copy(whole(src, s), whole(rp.at[k], s), p_send.at[k, 0, s], p_recv.at[k, s], partner(k)),
        )

    def send_offset(k, s, src, condition):
        send(
            even & condition,
            lambda: copy(upper(src, s), upper(ro.at[k], s), o_send.at[k, 0, s], o_recv.at[k, s], partner(k)),
        )

    def send_on(s, src, condition):
        send(
            even & condition & (group > 0),
            lambda: copy(upper(src, s), upper(rx, s), x_send.at[0, s], x_recv.at[s], me - size),
        )

    g_ref[second, :tail] = g_ref[first, third]
    g_ref[second, tail:2 * tail] = g_ref[second, third]

    for s in range(count):
        send(odd, lambda s=s: copy(whole(l_ref, s), whole(rp.at[0], s), p_send.at[0, 0, s], p_recv.at[0, s], me - 1))
    for s in range(count):
        send(odd, lambda s=s: copy(upper(g_ref, s), upper(ro.at[0], s), o_send.at[0, 0, s], o_recv.at[0, s], me - 1))

    @pl.when(even)
    def _():
        split(l_ref[...], ph, pll)
        arrive_factor(0)
        split(rp[0], vh, vl)

    for s in range(count):
        @pl.when(even)
        def _(s=s):
            factor_strip(sp.at[0], s)

        send_factor(1, s, sp.at[0], me >= 0)

    @pl.when(even)
    def _():
        for s in range(count):
            arrive_offset(0, s)
            split_strip(ro.at[0], s)

    for s in range(count):
        @pl.when(even)
        def _(s=s):
            fold_strip(g_ref, so.at[0], s)

        send_offset(1, s, so.at[0], me >= 0)

    send(me < n - 1, lambda: copy(l_ref, prev, n_send, n_recv, me + 1))

    @pl.when(odd)
    def _():
        so[0] = g_ref[...]
        sp[0] = l_ref[...]

    def own_phase(k, condition):
        early, late = bits[k] == 0, bits[k] == 1
        needed = wanted(k)
        same = even
        for b in range(1, k + 1):
            same = same & (bits[b] == 0)
        fold = condition & early & jnp.logical_not(same)

        @pl.when(condition & late)
        def _():
            so[k] = so[k - 1]
            sp[k] = sp[k - 1]

        @pl.when(condition & same)
        def _():
            so[k] = to[k]

        @pl.when(condition & same & needed)
        def _():
            sp[k] = tp[k]

        @pl.when(fold)
        def _():
            split(sp[k - 1], ph, pll)

        @pl.when(odd & fold & needed)
        def _():
            arrive_factor(k)

        @pl.when(fold & needed)
        def _():
            split(rp[k], vh, vl)
            for s in range(count):
                factor_strip(sp.at[k], s)

        @pl.when(odd & fold)
        def _():
            for s in range(count):
                arrive_offset(k, s)

        @pl.when(fold)
        def _():
            for s in range(count):
                split_strip(ro.at[k], s)
            for s in range(count):
                fold_strip(so.at[k - 1], so.at[k], s)

    inner = rest & even & (group > 0)

    for k in range(1, levels):
        early, late = bits[k] == 0, bits[k] == 1
        t_o = so.at[0] if k == 1 else to.at[k - 1]
        t_p = sp.at[0] if k == 1 else tp.at[k - 1]
        final = k == levels - 1
        needed = wanted(k)

        for s in range(count):
            @pl.when(even & (late | needed))
            def _(s=s):
                arrive(whole(rp.at[k], s), p_send.at[k, 0, s], p_recv.at[k, s])

            send(
                even & early & needed,
                lambda k=k, s=s: copy(whole(rp.at[k], s), whole(rp.at[k], s), p_send.at[k, 1, s], p_recv.at[k, s], me + 1),
            )

        @pl.when(even & early)
        def _():
            split(t_p[...], ph, pll)

        @pl.when(even & early & needed)
        def _():
            split(rp[k], vh, vl)

        @pl.when(even & late)
        def _():
            split(rp[k], ph, pll)
            split(t_p[...], vh, vl)

        for s in range(count):
            @pl.when(even & needed)
            def _(s=s):
                factor_strip(tp.at[k], s)

            if not final:
                send_factor(k + 1, s, tp.at[k], needed)

        @pl.when(even & late)
        def _():
            for s in range(count):
                split_strip(t_o, s)
            for s in range(count):
                fold_strip(None, xc, s)

        for s in range(count):
            @pl.when(even)
            def _(s=s):
                arrive_offset(k, s)

            send(
                even & early,
                lambda k=k, s=s: copy(upper(ro.at[k], s), upper(ro.at[k], s), o_send.at[k, 1, s], o_recv.at[k, s], me + 1),
            )

            @pl.when(even & early)
            def _(s=s):
                split_strip(ro.at[k], s)

            @pl.when(even & late)
            def _(s=s):
                upper(to.at[k], s)[...] = upper(ro.at[k], s)[...] + upper(xc, s)[...]

            if final:
                send_on(s, to.at[k], late & (group == top))
            else:
                send_offset(k + 1, s, to.at[k], late)

        for s in range(count):
            @pl.when(even & early)
            def _(s=s):
                fold_strip(t_o, to.at[k], s)

            if final:
                send_on(s, to.at[k], early & (group == top))
            else:
                send_offset(k + 1, s, to.at[k], early)

        own_phase(k, jnp.logical_not(inner) if final else me >= 0)

    last = levels - 1

    @pl.when(inner)
    def _():
        split(tp[last], ph, pll)

    @pl.when(rest & jnp.logical_not(inner))
    def _():
        split(sp[last], ph, pll)

    for s in range(count):
        @pl.when(rest)
        def _(s=s):
            arrive(upper(rx, s), x_send.at[0, s], x_recv.at[s])

        send(rest & even, lambda s=s: copy(upper(rx, s), upper(rx, s), x_send.at[1, s], x_recv.at[s], me + 1))

        @pl.when(rest)
        def _(s=s):
            split_strip(rx, s)

    for s in range(count):
        @pl.when(inner)
        def _(s=s):
            fold_strip(to.at[last], xc, s)

        send_on(s, xc, rest)

    own_phase(last, inner)

    @pl.when(inner)
    def _():
        split(sp[last], ph, pll)
        for s in range(count):
            split_strip(rx, s)

    @pl.when(rest)
    def _():
        for s in range(count):
            fold_strip(so.at[last], xt, s)

    @pl.when(group == top)
    def _():
        xt[...] = so[last]

    x_ref[first, :wide] = xt[first, :wide]
    x_ref[second, first] = xt[first, second].T
    x_ref[second, second] = xt[second, second]
    tails = xt[second, first]
    turned = tails.T
    x_ref[first, third] = tails[:, :tail]
    x_ref[second, third] = tails[:, tail:2 * tail]
    x_ref[third, first] = turned[:tail]
    x_ref[third, second] = turned[tail:2 * tail]
    x_ref[third, third] = xt[third, third]

    @pl.when(me > 0)
    def _():
        copy(prev, prev, n_send, n_recv, me).wait_recv()
        q_ref[...] = prev[...]

    @pl.when(me == 0)
    def _():
        q_ref[...] = jnp.zeros_like(q_ref)

    for condition, make in pending:
        @pl.when(condition)
        def _(make=make):
            make().wait_send()


def finish(x_ref, q_ref, d_ref, c_ref, xh, xl, qh, ql):
    d_ref[...] = x_ref[...]
    split(x_ref[...], xh, xl)
    split(q_ref[...], qh, ql)
    c_ref[...] = product((xh, xl), (qh, ql), NT)


def local(n, levels, schur_inverse, sweep_factor):
    order = schur_inverse.shape[1]
    full = (order, order)
    count = len(strips_of(order))
    f32, bf16 = jnp.float32, jnp.bfloat16
    dma = pltpu.SemaphoreType.DMA
    current, previous = pl.pallas_call(
        functools.partial(kernel, n, levels),
        out_shape=[jax.ShapeDtypeStruct(full, f32)] * 2,
        in_specs=[pl.BlockSpec(memory_space=pl.ANY)] * 2,
        out_specs=[pl.BlockSpec(memory_space=pltpu.VMEM)] * 2,
        scratch_shapes=[
            pltpu.VMEM(full, f32),
            pltpu.VMEM(full, f32),
            pltpu.VMEM((levels,) + full, f32),
            pltpu.VMEM((levels,) + full, f32),
            pltpu.VMEM((levels,) + full, f32),
            pltpu.VMEM((levels,) + full, f32),
            pltpu.VMEM((levels,) + full, f32),
            pltpu.VMEM((levels,) + full, f32),
            pltpu.VMEM(full, f32),
            pltpu.VMEM(full, f32),
            pltpu.VMEM(full, f32),
            pltpu.VMEM(full, f32),
        ] + [pltpu.VMEM(full, bf16)] * 6 + [
            dma((levels, levels + 1, count)), dma((levels, count)),
            dma((levels, levels + 1, count)), dma((levels, count)),
            dma((2, count)), dma((count,)), dma, dma, dma((2,)),
        ],
        compiler_params=pltpu.CompilerParams(
            collective_id=0, has_side_effects=True
        ),
    )(schur_inverse[0], sweep_factor[0])
    diagonal, coupling = pl.pallas_call(
        finish,
        out_shape=[jax.ShapeDtypeStruct(full, f32)] * 2,
        in_specs=[pl.BlockSpec(memory_space=pltpu.VMEM)] * 2,
        out_specs=[pl.BlockSpec(memory_space=pltpu.VMEM)] * 2,
        scratch_shapes=[pltpu.VMEM(full, bf16)] * 4,
    )(current, previous)
    return diagonal[None], coupling[None]


def solution(mesh):
    n = mesh.shape["tm"]
    levels = 0
    while levels < GROUP_LEVELS and n % (2 << levels) == 0:
        levels += 1
    return jax.shard_map(
        functools.partial(local, n, levels),
        mesh=mesh,
        in_specs=(P("tm", None, None), P("tm", None, None)),
        out_specs=(P("tm", None, None), P("tm", None, None)),
        check_vma=False,
    )
```

profile of v0, /device:TPU:5, one launch (start us, length us, event | category | flops | bytes accessed | tf_op | source)
XLA Modules:
  0.0 52.6 jit_solution(9973086489377833951)
XLA Ops:
  0.6 49.2 %shard_map.41 = (f32[320,320]{1,0:T(8,128)}, f32[320,320]{1,0:T(8,128)}) custom-call(f32[320,320]{1,0:T(8,128)} %bitcast.4, f32[320,320]{1,0:T(8,128)} %bitcast.5), custom_call_target="tpu_custom_call" | custom-call | tf_op jit(solution)/shard_map/pallas_call | solution.py:432
  49.9 2.7 %shard_map.42 = (f32[320,320]{1,0:T(8,128)}, f32[320,320]{1,0:T(8,128)}) custom-call(f32[320,320]{1,0:T(8,128)} %get-tuple-element.6.x_ref, f32[320,320]{1,0:T(8,128)} %get-tuple-element.7.q_ref), custom_call_target="tpu_custom_call" | custom-call | tf_op jit(solution)/shard_map/pallas_call | solution.py:459
where the time goes:
time: 52.8 us; the launch traced here: 52.6 us
  Pallas kernels  52 us (98%)
  between operations  0.64 us (1%)
    pallas_call x1, Pallas kernels, local(): pl.pallas_call(functools.partial(kernel, n, levels), out_shape=[jax.Shape...  49.2 us
    pallas_call x1, Pallas kernels, local(): pl.pallas_call(finish, out_shape=[jax.ShapeDtypeStruct(full, f32)] * 2, i...  2.72 us

commit v1 on v0

--- a/solution.py
+++ b/solution.py
@@ -416,11 +416,16 @@
             make().wait_send()
 
 
-def finish(x_ref, q_ref, d_ref, c_ref, xh, xl, qh, ql):
-    d_ref[...] = x_ref[...]
+def finish(x_ref, q_ref, d_any, c_any, c_ref, xh, xl, qh, ql, sem):
+    d_out = pltpu.make_async_copy(x_ref, d_any, sem.at[0])
+    d_out.start()
     split(x_ref[...], xh, xl)
     split(q_ref[...], qh, ql)
     c_ref[...] = product((xh, xl), (qh, ql), NT)
+    c_out = pltpu.make_async_copy(c_ref, c_any, sem.at[1])
+    c_out.start()
+    d_out.wait()
+    c_out.wait()
 
 
 def local(n, levels, schur_inverse, sweep_factor):
@@ -431,7 +436,7 @@
     dma = pltpu.SemaphoreType.DMA
     current, previous = pl.pallas_call(
         functools.partial(kernel, n, levels),
-        out_shape=[jax.ShapeDtypeStruct(full, f32)] * 2,
+        out_shape=[pltpu.VMEM(full, f32)] * 2,
         in_specs=[pl.BlockSpec(memory_space=pl.ANY)] * 2,
         out_specs=[pl.BlockSpec(memory_space=pltpu.VMEM)] * 2,
         scratch_shapes=[
@@ -460,9 +465,9 @@
         finish,
         out_shape=[jax.ShapeDtypeStruct(full, f32)] * 2,
         in_specs=[pl.BlockSpec(memory_space=pltpu.VMEM)] * 2,
-        out_specs=[pl.BlockSpec(memory_space=pltpu.VMEM)] * 2,
-        scratch_shapes=[pltpu.VMEM(full, bf16)] * 4,
-    )(current, previous)
+        out_specs=[pl.BlockSpec(memory_space=pl.ANY)] * 2,
+        scratch_shapes=[pltpu.VMEM(full, f32)] + [pltpu.VMEM(full, bf16)] * 4 + [dma((2,))],
+    )(*(pltpu.with_memory_space_constraint(v, pltpu.VMEM) for v in (current, previous)))
     return diagonal[None], coupling[None]
 
 

time: 52.8 us -> 50.7 us (0.960)
  Pallas kernels: 52 us -> 49.7 us
    pallas_call x1, Pallas kernels: 2.72 us -> 1.43 us  [local(): pl.pallas_call(finish, out_shape=[jax.ShapeDtypeStruct(full, f32)] * 2, i...]
    pallas_call x1, Pallas kernels: 49.2 us -> 48.3 us  [local(): pl.pallas_call(functools.partial(kernel, n, levels), out_shape=[pltpu.VME...]
where the time goes in v1:
time: 50.7 us; the launch traced here: 50.5 us
  Pallas kernels  49.7 us (98%)
  between operations  0.8 us (2%)
    pallas_call x1, Pallas kernels, local(): pl.pallas_call(functools.partial(kernel, n, levels), out_shape=[pltpu.VME...  48.3 us
    pallas_call x1, Pallas kernels, local(): pl.pallas_call(finish, out_shape=[jax.ShapeDtypeStruct(full, f32)] * 2, i...  1.43 us

profile of v1, /device:TPU:5, one launch (start us, length us, event | category | flops | bytes accessed | tf_op | source)
XLA Modules:
  0.0 50.5 jit_solution(4297095519814823361)
XLA Ops:
  0.6 48.3 %shard_map.41 = (f32[320,320]{1,0:T(8,128)S(1)}, f32[320,320]{1,0:T(8,128)S(1)}) custom-call(f32[320,320]{1,0:T(8,128)} %bitcast.4, f32[320,320]{1,0:T(8,128)} %bitcast.5), custom_call_target="tpu_custom_call" | custom-call | tf_op jit(solution)/shard_map/pallas_call | solution.py:437
  48.9 1.4 %shard_map.42 = (f32[320,320]{1,0:T(8,128)}, f32[320,320]{1,0:T(8,128)}) custom-call(f32[320,320]{1,0:T(8,128)S(1)} %get-tuple-element.6.x_ref, f32[320,320]{1,0:T(8,128)S(1)} %get-tuple-element.7.q_ref), custom_call_target="tpu_custom_call" | custom-call | tf_op jit(solution)/shard_map/pallas_call | solution.py:464

commit v2 on v1

v2 whole, which is shorter than its diff:
```python
import functools

import jax
import jax.numpy as jnp
from jax import lax
from jax.experimental import pallas as pl
from jax.experimental.pallas import tpu as pltpu
from jax.sharding import PartitionSpec as P

MESH = pl.DeviceIdType.MESH
STRIP = 128
WIDE = 2 * STRIP
GROUP = 8
NN = (((1,), (0,)), ((), ()))
NT = (((1,), (1,)), ((), ()))

OWN, PAIR, ALL, LAST, XF, YF, ZF, LOW = range(8)
CHAIN, EVEN, XO, YO, LOWO, EDGE, ZO, BASE = range(3, 11)
SL, SM, SC, SX, SY, SP, SA, SB, SR, SZ, SW = range(11)
DIAG, EDGE2 = 11, 12


def dot(left, right, dims):
    return lax.dot_general(left, right, dims, preferred_element_type=jnp.float32)


def split(value, high, low):
    top = value.astype(jnp.bfloat16)
    high[...] = top
    low[...] = (value - top.astype(jnp.float32)).astype(jnp.bfloat16)


def product(left, right, dims):
    lh, ll = left
    rh, rl = right
    return (
        dot(lh[...], rl[...], dims) + dot(ll[...], rh[...], dims)
    ) + dot(lh[...], rh[...], dims)


def kernel(n, g_any, l_any, x_ref, q_ref, *scratch):
    (g_ref, l_ref, other, prev, acc, pm, pt, so, high, low,
     p_send, p_recv, s_send, s_recv, l_send, l_recv, n_send, n_recv, in_sem, turn) = scratch
    order = g_ref.shape[0]
    half = order // 2
    tail = order - WIDE
    groups = n // GROUP
    joined = groups >= 3
    me = lax.axis_index("tm")
    j = lax.rem(me, GROUP)
    group = me // GROUP
    b0, b1, b2 = (lax.rem(j // d, 2) for d in (1, 2, 4))
    even, odd = b0 == 0, b0 == 1
    chip = j // 2
    xe, xl, ye, yl = b1 == 0, b1 == 1, b2 == 0, b2 == 1
    top = group == groups - 1
    rest = group < groups - 1
    bottom = (group == 0) & joined
    chain = rest & (group >= (2 if joined else 1))
    core = me + 1 - 2 * b0
    px = me + 2 - 4 * b1
    py = me + 4 - 8 * b2

    g_in = pltpu.make_async_copy(g_any, g_ref, in_sem.at[0])
    l_in = pltpu.make_async_copy(l_any, l_ref, in_sem.at[1])
    l_in.start()
    g_in.start()

    barrier = pltpu.get_barrier_semaphore()
    total = 0
    always = me >= 0
    for other_id, inside in (
        (core, always), (px, always), (py, always),
        (me + 2, odd & top & (chip == 1)), (me - 2, odd & top & (chip == 2)),
        (me - GROUP, group > 0), (me + GROUP, rest),
        (me - 2 * GROUP, odd & (group == 2)), (me + 2 * GROUP, odd & (group == 0) & (groups > 2)),
        (me - GROUP + 4, odd & top & ye & (group > 0)), (me + GROUP - 4, odd & yl & (group == groups - 2)),
        (me - 2 * GROUP + 4, odd & top & ye & (group == 2)),
        (me + 2 * GROUP - 4, odd & yl & (group == 0) & (groups == 3)),
        (me + 1, odd & (me < n - 1)), (me - 1, even & (me > 0)),
    ):
        total = total + inside.astype(jnp.int32)

        @pl.when(inside)
        def _(other_id=other_id):
            pl.semaphore_signal(barrier, inc=1, device_id=(other_id,), device_id_type=MESH)

    first, second, third = slice(0, STRIP), slice(STRIP, WIDE), slice(WIDE, order)
    left, right = slice(0, tail), slice(tail, 2 * tail)

    def slot(i, a=0, b=order):
        return high.at[i, a:b, :], low.at[i, a:b, :]

    def fill(i, value):
        split(value, *slot(i))

    def copy(src, dst, send, recv, target):
        return pltpu.make_async_remote_copy(
            src_ref=src, dst_ref=dst, send_sem=send, recv_sem=recv,
            device_id=(target,), device_id_type=MESH,
        )

    pending = []

    def send(condition, make, wait=True):
        @pl.when(condition)
        def _():
            make().start()
        if wait:
            pending.append((condition, make))

    def factor(i):
        return pm.at[i, :half, :WIDE], pm.at[i, half:, :WIDE], pt.at[i]

    def offset(i):
        return so.at[i, first, :], so.at[i, second, :]

    def send_factor(condition, src, dst, target, parts=(0, 1, 2), wait=True, sem=None):
        sem = dst if sem is None else sem
        for s in parts:
            send(
                condition,
                lambda s=s: copy(factor(src)[s], factor(dst)[s], p_send.at[sem, s], p_recv.at[dst, s], target),
                wait,
            )

    def sent_factor(condition, dst):
        @pl.when(condition)
        def _():
            for s in range(3):
                copy(factor(dst)[s], factor(dst)[s], p_send.at[dst, s], p_recv.at[dst, s], core).wait_send()

    def send_offset(condition, src, dst, target, parts=(0, 1), sem=None):
        sem = dst if sem is None else sem
        for s in parts:
            send(
                condition,
                lambda s=s: copy(offset(src)[s], offset(dst)[s], s_send.at[sem, s], s_recv.at[dst, s], target),
            )

    def got_factor(i):
        for s, ref in enumerate(factor(i)):
            copy(ref, ref, p_send.at[i, s], p_recv.at[i, s], me).wait_recv()

    def got_offset(i, s):
        ref = offset(i)[s]
        copy(ref, ref, s_send.at[i, s], s_recv.at[i, s], me).wait_recv()

    def got_offsets(i):
        got_offset(i, 0)
        got_offset(i, 1)

    def load_factor(i, k):
        h, l = high.at[k], low.at[k]
        split(pm[i, :, :WIDE], h.at[:, :WIDE], l.at[:, :WIDE])
        ends = pt[i]
        split(ends[:, :tail], h.at[:half, third], l.at[:half, third])
        split(ends[:, tail:2 * tail], h.at[half:, third], l.at[half:, third])

    def multiply(i, k, r, out, into=None):
        rows = slice(i * half, (i + 1) * half)
        value = product(slot(k, rows.start, rows.stop), slot(r), NN)
        if out is not None:
            pm[out, rows, :WIDE] = value[:, :WIDE]
            pt[out, :, i * tail:(i + 1) * tail] = value[:, third]
        if into is not None:
            split(value, *slot(into, rows.start, rows.stop))

    def pack(ref, i):
        so[i, first, :] = ref[first, :WIDE]
        so[i, second, left] = ref[first, third]
        so[i, second, right] = ref[second, third]
        so[i, STRIP:STRIP + tail, second] = ref[STRIP:STRIP + tail, second]
        so[i, STRIP + tail:WIDE, STRIP + tail:] = ref[STRIP + tail:WIDE, STRIP + tail:WIDE]
        so[i, STRIP + tail:WIDE, STRIP:STRIP + tail] = ref[third, third]

    def spread(i, put, parts=(0, 1)):
        if 0 in parts:
            put(so[i, first, :], first, slice(0, WIDE))
            put(so[i, first, second].T, second, first)
        if 1 in parts:
            ends = so[i, second, first]
            turned = ends.T
            put(ends[:, :tail], first, third)
            put(ends[:, tail:2 * tail], second, third)
            put(turned[:tail], third, first)
            put(turned[tail:2 * tail], third, second)
            block = so[i, second, second]
            lanes = lax.broadcasted_iota(jnp.int32, (STRIP - tail, STRIP), 1)
            put(block[:tail], slice(STRIP, STRIP + tail), second)
            put(jnp.where(lanes < tail, block.T[tail:], block[tail:]), slice(STRIP + tail, WIDE), second)
            put(block[tail:, :tail], third, third)

    def to_slot(k):
        def put(value, rows, columns):
            split(value, high.at[k, rows, columns], low.at[k, rows, columns])
        return put

    def to_ref(ref):
        def put(value, rows, columns):
            ref[rows, columns] = value
        return put

    def fold_strip(s, k, base, out):
        a, b = ((0, STRIP), (STRIP, order))[s]
        split(product(slot(k, a, b), slot(SZ), NN), *slot(SW, a, b))
        term = product(slot(SW, a, b), slot(k, a), NT)
        if s == 0:
            so[out, first, :] = so[base, first, :] + term[:, :WIDE]
            so[out, second, left] = so[base, second, left] + term[:, WIDE:]
        else:
            lower = slice(STRIP + tail, WIDE)
            so[out, second, right] = so[base, second, right] + term[:STRIP, STRIP:]
            so[out, STRIP:STRIP + tail, second] = so[base, STRIP:STRIP + tail, second] + term[:tail, :STRIP]
            so[out, lower, lower] = so[base, lower, lower] + term[tail:STRIP, tail:STRIP]
            so[out, lower, STRIP:STRIP + tail] = so[base, lower, STRIP:STRIP + tail] + term[STRIP:, STRIP:]

    def fold(condition, k, base, out, after=None):
        for s in range(2):
            @pl.when(condition)
            def _(s=s):
                fold_strip(s, k, base, out)
            if after is not None:
                after(s)

    def fold_whole(k, base, out):
        fill(SW, product(slot(k), slot(SZ), NN))
        out[...] = base[...] + product(slot(SW), slot(k), NT)

    l_in.wait()

    @pl.when(even)
    def _():
        fill(SL, l_ref[...])

    @pl.when(odd)
    def _():
        fill(SM, l_ref[...])

    g_in.wait()

    @pl.when(even)
    def _():
        pack(g_ref, BASE)

    @pl.when(odd)
    def _():
        fill(SZ, g_ref[...])

    pl.semaphore_wait(barrier, total)

    send(always, lambda: copy(l_ref, other, l_send, l_recv, core))
    send_offset(even, BASE, BASE, core)

    swap_x = even & (rest | ye)

    copy(other, other, l_send, l_recv, me).wait_recv()

    @pl.when(even)
    def _():
        fill(SM, other[...])

    for i in range(2):
        @pl.when(even)
        def _(i=i):
            multiply(i, SL, SM, OWN, SC)
        send_factor(swap_x, OWN, XF, px, (i,), wait=False)
    send_factor(swap_x, OWN, XF, px, (2,), wait=False)

    @pl.when(odd)
    def _():
        fill(SL, other[...])
        got_offsets(BASE)

    early_o = odd & top & ((chip == 1) | (chip == 3))
    fold(odd, SL, BASE, OWN, lambda s: send_offset(early_o, OWN, XO, px, (s,)))

    @pl.when(odd)
    def _():
        for i in range(2):
            multiply(i, SL, SM, None, SC)

    sent_factor(swap_x, XF)

    @pl.when(even & rest)
    def _():
        pl.semaphore_signal(turn.at[0], inc=1, device_id=(core,), device_id_type=MESH)

    @pl.when(odd & rest)
    def _():
        pl.semaphore_wait(turn.at[0], 1)

    send_offset(odd & rest, OWN, XO, px)

    @pl.when(swap_x)
    def _():
        got_factor(XF)

    send_factor(swap_x, XF, LOW, core)

    @pl.when(swap_x)
    def _():
        load_factor(XF, SX)

    def ordered(condition, early, k, r, a, b):
        @pl.when(condition & early)
        def _():
            high[a], low[a], high[b], low[b] = high[k], low[k], high[r], low[r]

        @pl.when(condition & jnp.logical_not(early))
        def _():
            high[a], low[a], high[b], low[b] = high[r], low[r], high[k], low[k]

    ordered(swap_x, xe, SC, SX, SA, SB)
    swap_y = even & rest
    for i in range(2):
        @pl.when(swap_x)
        def _(i=i):
            multiply(i, SA, SB, PAIR, SP)
        send_factor(swap_y, PAIR, YF, py, (i,), wait=False)
    send_factor(swap_y, PAIR, YF, py, (2,), wait=False)
    send_factor(swap_x & ye, PAIR, ZF, core)

    o_fold = odd & (rest | (chip == 0) | (chip == 2))

    @pl.when(odd & (rest | ye))
    def _():
        got_factor(LOW)
        load_factor(LOW, SX)

    @pl.when(o_fold)
    def _():
        got_offsets(XO)

    @pl.when(o_fold & xe)
    def _():
        spread(XO, to_slot(SZ))
        high[SA], low[SA] = high[SC], low[SC]
        so[BASE] = so[OWN]

    @pl.when(o_fold & xl)
    def _():
        spread(OWN, to_slot(SZ))
        high[SA], low[SA] = high[SX], low[SX]
        so[BASE] = so[XO]

    def after_pair(s):
        send_offset(odd & top & (chip == 2), PAIR, YO, py, (s,))
        send_offset(odd & top & (chip == 2), PAIR, YO, me - 2, (s,), DIAG)
        send_offset(odd & top & (chip == 0), PAIR, LOWO, px, (s,))

    fold(o_fold, SA, BASE, PAIR, after_pair)

    sent_factor(swap_y, YF)

    @pl.when(swap_y)
    def _():
        pl.semaphore_signal(turn.at[1], inc=1, device_id=(core,), device_id_type=MESH)

    @pl.when(odd & rest)
    def _():
        pl.semaphore_wait(turn.at[1], 1)

    send_offset(odd & rest, PAIR, YO, py)

    @pl.when(swap_y)
    def _():
        got_factor(YF)

    send_factor(swap_y & yl, YF, ZF, core)

    @pl.when(swap_y)
    def _():
        load_factor(YF, SY)

    ordered(swap_y, ye, SP, SY, SA, SB)
    down = even & (group == 1) & rest & joined
    for i in range(2):
        @pl.when(swap_y)
        def _(i=i):
            multiply(i, SA, SB, ALL, SR)
        send_factor(down, ALL, ZF, me - GROUP, (i,), sem=OWN)
    send_factor(down, ALL, ZF, me - GROUP, (2,), sem=OWN)
    send_factor(even & chain, ALL, ALL, core)

    @pl.when(swap_y & (chip == 0))
    def _():
        for i in range(2):
            multiply(i, SX, SY, None, SB)
        high[SA], low[SA] = high[SR], low[SR]

    @pl.when(swap_y & (chip == 1))
    def _():
        for i in range(2):
            multiply(i, SC, SY, None, SA)
        high[SB], low[SB] = high[SY], low[SY]

    @pl.when(swap_y & (chip == 2))
    def _():
        high[SA], low[SA] = high[SP], low[SP]
        high[SB], low[SB] = high[SX], low[SX]

    @pl.when(swap_y & (chip == 3))
    def _():
        high[SA], low[SA] = high[SC], low[SC]

    hand = swap_y & (chip < 3)

    @pl.when(hand)
    def _():
        for i in range(2):
            multiply(i, SM, SB, LAST)

    send_factor(hand, LAST, LAST, core)

    z_fold = odd & (rest | ye)

    @pl.when(z_fold)
    def _():
        got_factor(ZF)
        load_factor(ZF, SP)

    @pl.when(odd & top & (chip == 1))
    def _():
        got_offsets(LOWO)

    @pl.when(z_fold)
    def _():
        got_offsets(YO)

    @pl.when(odd & rest & yl)
    def _():
        spread(PAIR, to_slot(SZ))
        so[BASE] = so[YO]

    @pl.when(z_fold & ye)
    def _():
        spread(YO, to_slot(SZ))

    @pl.when(odd & ye & (rest | (chip == 0)))
    def _():
        so[BASE] = so[PAIR]

    @pl.when(odd & top & (chip == 1))
    def _():
        so[BASE] = so[LOWO]

    far = group == 2 if joined else me < 0
    near = (group >= 2) if joined else (group >= 1)

    def after_all(s):
        send_offset(odd & top & ye & near, ALL, EDGE, me - GROUP, (s,))
        send_offset(odd & top & ye & far, ALL, EDGE, me - 2 * GROUP, (s,), ZO)

    fold(z_fold, SP, BASE, ALL, after_all)
    send_offset(odd & top & ye & near, ALL, EDGE, me - GROUP + 4, (0, 1), EDGE2)
    send_offset(odd & top & ye & far, ALL, EDGE, me - 2 * GROUP + 4, (0, 1), DIAG)
    send_offset(odd & rest & (group == 1) & joined, ALL, ZO, me - GROUP)

    @pl.when(odd & chain)
    def _():
        got_factor(ALL)
        load_factor(ALL, SR)

    for s in range(2):
        @pl.when(odd & chain)
        def _(s=s):
            got_offset(EDGE, s)
        send_offset(odd & chain, EDGE, EDGE, core, (s,), CHAIN)

        @pl.when(odd & chain)
        def _(s=s):
            spread(EDGE, to_slot(SZ), (s,))

    def after_chain(s):
        send_offset(odd & chain & far, CHAIN, EDGE, me - 2 * GROUP, (s,), EDGE2)
        send_offset(odd & chain & near, CHAIN, EDGE, me - GROUP, (s,))

    fold(odd & chain, SR, ALL, CHAIN, after_chain)
    send(odd & (me < n - 1), lambda: copy(l_ref, prev, n_send, n_recv, me + 1))

    send_offset(odd & (chip == 0), ALL, EVEN, core)
    send_offset(odd & (chip == 2), PAIR, EVEN, core)
    send_offset(odd & (chip == 3), OWN, EVEN, core)
    low_y = odd & ye

    @pl.when(low_y)
    def _():
        spread(YO, to_slot(SZ))

    @pl.when(low_y & (chip == 1))
    def _():
        high[SA], low[SA] = high[SC], low[SC]
        so[BASE] = so[OWN]

    @pl.when(low_y & (chip == 0))
    def _():
        high[SA], low[SA] = high[SX], low[SX]
        so[BASE] = so[XO]

    fold(low_y, SA, BASE, EVEN)
    send_offset(odd & (chip == 1), EVEN, EVEN, core)

    @pl.when(odd & (chip == 0))
    def _():
        spread(EVEN, to_slot(SZ))

    @pl.when(odd & (chip == 1))
    def _():
        spread(YO, to_slot(SZ))

    @pl.when(odd & (chip == 2))
    def _():
        spread(XO, to_slot(SZ))

    @pl.when(odd & (chip < 3))
    def _():
        fold_whole(SM, g_ref, acc)

    @pl.when(odd & (chip == 3))
    def _():
        acc[...] = g_ref[...]

    @pl.when(odd & rest & (chip < 3))
    def _():
        got_factor(LAST)
        load_factor(LAST, SA)

    @pl.when(odd & rest & (chip == 3))
    def _():
        high[SA], low[SA] = high[SM], low[SM]

    @pl.when(even)
    def _():
        got_offsets(EVEN)
        spread(EVEN, to_ref(acc))

    @pl.when(bottom & even)
    def _():
        got_factor(ZF)

    send_factor(bottom & even, ZF, YF, core)

    @pl.when(bottom & even)
    def _():
        load_factor(ZF, SR)

    @pl.when(bottom & odd)
    def _():
        got_factor(YF)
        load_factor(YF, SR)

    @pl.when(bottom)
    def _():
        for i in range(2):
            multiply(i, SA, SR, None, SB)
        got_offsets(ZO)

    send_offset(bottom & odd, ZO, ZO, core)

    @pl.when(bottom)
    def _():
        spread(ZO, to_slot(SZ))
        fold_whole(SA, acc, acc)
        high[SA], low[SA] = high[SB], low[SB]

    @pl.when(odd)
    def _():
        q_ref[...] = other[...]

    @pl.when(even & (me > 0))
    def _():
        copy(prev, prev, n_send, n_recv, me).wait_recv()
        q_ref[...] = prev[...]

    @pl.when(me == 0)
    def _():
        q_ref[...] = jnp.zeros_like(q_ref)

    for s in range(2):
        @pl.when(rest & (even | jnp.logical_not(chain)))
        def _(s=s):
            got_offset(EDGE, s)

        send_offset(rest & odd & jnp.logical_not(chain), EDGE, EDGE, core, (s,), CHAIN)

        @pl.when(rest)
        def _(s=s):
            spread(EDGE, to_slot(SZ), (s,))

    @pl.when(rest)
    def _():
        fold_whole(SA, acc, x_ref)

    @pl.when(top)
    def _():
        x_ref[...] = acc[...]

    for condition, make in pending:
        @pl.when(condition)
        def _(make=make):
            make().wait_send()


def finish(x_ref, q_ref, d_any, c_any, c_ref, xh, xl, qh, ql, sem):
    d_out = pltpu.make_async_copy(x_ref, d_any, sem.at[0])
    d_out.start()
    split(x_ref[...], xh, xl)
    split(q_ref[...], qh, ql)
    c_ref[...] = product((xh, xl), (qh, ql), NT)
    c_out = pltpu.make_async_copy(c_ref, c_any, sem.at[1])
    c_out.start()
    d_out.wait()
    c_out.wait()


def local(n, schur_inverse, sweep_factor):
    order = schur_inverse.shape[1]
    full = (order, order)
    f32, bf16 = jnp.float32, jnp.bfloat16
    dma = pltpu.SemaphoreType.DMA
    current, previous = pl.pallas_call(
        functools.partial(kernel, n),
        out_shape=[pltpu.VMEM(full, f32)] * 2,
        in_specs=[pl.BlockSpec(memory_space=pl.ANY)] * 2,
        out_specs=[pl.BlockSpec(memory_space=pltpu.VMEM)] * 2,
        scratch_shapes=[pltpu.VMEM(full, f32)] * 5 + [
            pltpu.VMEM((8,) + full, f32),
            pltpu.VMEM((8, order // 2, STRIP), f32),
            pltpu.VMEM((11, WIDE, WIDE), f32),
            pltpu.VMEM((11,) + full, bf16),
            pltpu.VMEM((11,) + full, bf16),
            dma((8, 3)), dma((8, 3)), dma((13, 2)), dma((13, 2)),
            dma, dma, dma, dma, dma((2,)), pltpu.SemaphoreType.REGULAR((2,)),
        ],
        compiler_params=pltpu.CompilerParams(
            collective_id=0, has_side_effects=True
        ),
    )(schur_inverse[0], sweep_factor[0])
    diagonal, coupling = pl.pallas_call(
        finish,
        out_shape=[jax.ShapeDtypeStruct(full, f32)] * 2,
        in_specs=[pl.BlockSpec(memory_space=pltpu.VMEM)] * 2,
        out_specs=[pl.BlockSpec(memory_space=pl.ANY)] * 2,
        scratch_shapes=[pltpu.VMEM(full, f32)] + [pltpu.VMEM(full, bf16)] * 4 + [dma((2,))],
    )(*(pltpu.with_memory_space_constraint(v, pltpu.VMEM) for v in (current, previous)))
    return diagonal[None], coupling[None]


def solution(mesh):
    n = mesh.shape["tm"]
    return jax.shard_map(
        functools.partial(local, n),
        mesh=mesh,
        in_specs=(P("tm", None, None), P("tm", None, None)),
        out_specs=(P("tm", None, None), P("tm", None, None)),
        check_vma=False,
    )
```

time: 50.7 us -> 43.9 us (0.87)
  the two profiles are of different devices: /device:TPU:5 before, /device:TPU:14 now
where the time goes in v2:
time: 43.9 us; the launch traced here: 43.8 us
  Pallas kernels  43 us (98%)
  between operations  0.8 us (2%)
    pallas_call x1, Pallas kernels, local(): pl.pallas_call(functools.partial(kernel, n), out_shape=[pltpu.VMEM(full,...  41.5 us
    pallas_call x1, Pallas kernels, local(): pl.pallas_call(finish, out_shape=[jax.ShapeDtypeStruct(full, f32)] * 2, i...  1.42 us

profile of v2, /device:TPU:14, one launch (start us, length us, event | category | flops | bytes accessed | tf_op | source)
XLA Modules:
  0.0 43.8 jit_solution(17318703795766204834)
XLA Ops:
  0.6 41.5 %shard_map.41 = (f32[320,320]{1,0:T(8,128)S(1)}, f32[320,320]{1,0:T(8,128)S(1)}) custom-call(f32[320,320]{1,0:T(8,128)} %bitcast.4, f32[320,320]{1,0:T(8,128)} %bitcast.5), custom_call_target="tpu_custom_call" | custom-call | tf_op jit(solution)/shard_map/pallas_call | solution.py:622
  42.2 1.4 %shard_map.42 = (f32[320,320]{1,0:T(8,128)}, f32[320,320]{1,0:T(8,128)}) custom-call(f32[320,320]{1,0:T(8,128)S(1)} %get-tuple-element.6.x_ref, f32[320,320]{1,0:T(8,128)S(1)} %get-tuple-element.7.q_ref), custom_call_target="tpu_custom_call" | custom-call | tf_op jit(solution)/shard_map/pallas_call | solution.py:640

commit v3 on v2

--- a/solution.py
+++ b/solution.py
@@ -15,9 +15,13 @@
 NT = (((1,), (1,)), ((), ()))
 
 OWN, PAIR, ALL, LAST, XF, YF, ZF, LOW = range(8)
-CHAIN, EVEN, XO, YO, LOWO, EDGE, ZO, BASE = range(3, 11)
+CHAIN, EVEN, XO, YO, EDGE, ZO, BASE = range(3, 10)
 SL, SM, SC, SX, SY, SP, SA, SB, SR, SZ, SW = range(11)
-DIAG, EDGE2 = 11, 12
+E_BASE, E_X, E_X2, E_LOW, E_PAIR, E_Y, E_Y2, E_ALL, E_LAST = range(9)
+O_X, O_Y, O_TO, O_NEAR, O_NEAR2, O_FAR, O_FAR2, O_Z, O_EVEN = range(9)
+R_FACTOR = {XF: 0, YF: 1, ZF: 2, LOW: 0, ALL: 3, LAST: 4}
+R_OFFSET = {BASE: 5, EVEN: 5, XO: 6, YO: 7, ZO: 8, EDGE: 9}
+PARTS = 4
 
 
 def dot(left, right, dims):
@@ -39,8 +43,8 @@
 
 
 def kernel(n, g_any, l_any, x_ref, q_ref, *scratch):
-    (g_ref, l_ref, other, prev, acc, pm, pt, so, high, low,
-     p_send, p_recv, s_send, s_recv, l_send, l_recv, n_send, n_recv, in_sem, turn) = scratch
+    (g_ref, l_ref, other, prev, acc, pm, pt, so, high, low, tally,
+     sent, got, l_send, l_recv, n_send, n_recv, in_sem, turn) = scratch
     order = g_ref.shape[0]
     half = order // 2
     tail = order - WIDE
@@ -102,53 +106,69 @@
 
     pending = []
 
-    def send(condition, make, wait=True):
+    def start(condition, make):
         @pl.when(condition)
         def _():
             make().start()
-        if wait:
-            pending.append((condition, make))
+
+    def send(condition, make):
+        start(condition, make)
+        pending.append((condition, make))
+
+    def drain():
+        for condition, make in pending:
+            @pl.when(condition)
+            def _(make=make):
+                make().wait_send()
+        pending.clear()
 
     def factor(i):
         return pm.at[i, :half, :WIDE], pm.at[i, half:, :WIDE], pt.at[i]
 
-    def offset(i):
-        return so.at[i, first, :], so.at[i, second, :]
-
-    def send_factor(condition, src, dst, target, parts=(0, 1, 2), wait=True, sem=None):
-        sem = dst if sem is None else sem
+    def quarter(s, count=1):
+        return slice(s * WIDE // PARTS, (s + count) * WIDE // PARTS)
+
+    def leave(condition, ref, sem):
+        pending.append((condition, lambda: copy(ref, ref, sent.at[sem], got.at[0], core)))
+
+    def send_factor(condition, src, dst, target, sem, parts=(0, 1, 2), ends=None):
         for s in parts:
-            send(
+            start(
                 condition,
-                lambda s=s: copy(factor(src)[s], factor(dst)[s], p_send.at[sem, s], p_recv.at[dst, s], target),
-                wait,
+                lambda s=s: copy(
+                    factor(src)[s], factor(dst)[s],
+                    sent.at[ends if s == 2 and ends is not None else sem], got.at[R_FACTOR[dst]], target,
+                ),
             )
-
-    def sent_factor(condition, dst):
+        if 2 in parts and ends is None:
+            leave(condition, tally, sem)
+
+    def send_offset(condition, src, dst, target, sem, parts=range(PARTS), count=PARTS):
+        for s in parts:
+            start(
+                condition,
+                lambda s=s: copy(
+                    so.at[src, quarter(s), :], so.at[dst, quarter(s), :],
+                    sent.at[sem], got.at[R_OFFSET[dst] + (s if dst == EDGE else 0)], target,
+                ),
+            )
+        if PARTS - 1 in parts:
+            leave(condition, so.at[src, quarter(0, count), :], sem)
+
+    def wait_sent(condition, ref, sem):
         @pl.when(condition)
         def _():
-            for s in range(3):
-                copy(factor(dst)[s], factor(dst)[s], p_send.at[dst, s], p_recv.at[dst, s], core).wait_send()
-
-    def send_offset(condition, src, dst, target, parts=(0, 1), sem=None):
-        sem = dst if sem is None else sem
-        for s in parts:
-            send(
-                condition,
-                lambda s=s: copy(offset(src)[s], offset(dst)[s], s_send.at[sem, s], s_recv.at[dst, s], target),
-            )
+            copy(ref, ref, sent.at[sem], got.at[0], core).wait_send()
 
     def got_factor(i):
-        for s, ref in enumerate(factor(i)):
-            copy(ref, ref, p_send.at[i, s], p_recv.at[i, s], me).wait_recv()
-
-    def got_offset(i, s):
-        ref = offset(i)[s]
-        copy(ref, ref, s_send.at[i, s], s_recv.at[i, s], me).wait_recv()
-
-    def got_offsets(i):
-        got_offset(i, 0)
-        got_offset(i, 1)
+        copy(tally, tally, sent.at[0], got.at[R_FACTOR[i]], me).wait_recv()
+
+    def got_offset(i):
+        copy(so.at[i], so.at[i], sent.at[0], got.at[R_OFFSET[i]], me).wait_recv()
+
+    def got_edge(s):
+        ref = so.at[EDGE, quarter(s), :]
+        copy(ref, ref, sent.at[0], got.at[R_OFFSET[EDGE] + s], me).wait_recv()
 
     def load_factor(i, k):
         h, l = high.at[k], low.at[k]
@@ -201,9 +221,12 @@
             ref[rows, columns] = value
         return put
 
-    def fold_strip(s, k, base, out):
+    def fold_left(s, k):
         a, b = ((0, STRIP), (STRIP, order))[s]
         split(product(slot(k, a, b), slot(SZ), NN), *slot(SW, a, b))
+
+    def fold_right(s, k, base, out):
+        a, b = ((0, STRIP), (STRIP, order))[s]
         term = product(slot(SW, a, b), slot(k, a), NT)
         if s == 0:
             so[out, first, :] = so[base, first, :] + term[:, :WIDE]
@@ -215,17 +238,25 @@
             so[out, lower, lower] = so[base, lower, lower] + term[tail:STRIP, tail:STRIP]
             so[out, lower, STRIP:STRIP + tail] = so[base, lower, STRIP:STRIP + tail] + term[STRIP:, STRIP:]
 
-    def fold(condition, k, base, out, after=None):
+    def fold(condition, k, base, out, after):
         for s in range(2):
             @pl.when(condition)
             def _(s=s):
-                fold_strip(s, k, base, out)
-            if after is not None:
-                after(s)
+                fold_left(s, k)
+                fold_right(s, k, base, out)
+            after(s)
+
+    def fold_at_once(k, base, out):
+        fold_left(0, k)
+        fold_left(1, k)
+        fold_right(0, k, base, out)
+        fold_right(1, k, base, out)
 
     def fold_whole(k, base, out):
-        fill(SW, product(slot(k), slot(SZ), NN))
-        out[...] = base[...] + product(slot(SW), slot(k), NT)
+        for a in (0, half):
+            split(product(slot(k, a, a + half), slot(SZ), NN), *slot(SW, a, a + half))
+        for a in (0, half):
+            out[a:a + half, :] = base[a:a + half, :] + product(slot(SW, a, a + half), slot(k), NT)
 
     l_in.wait()
 
@@ -250,7 +281,7 @@
     pl.semaphore_wait(barrier, total)
 
     send(always, lambda: copy(l_ref, other, l_send, l_recv, core))
-    send_offset(even, BASE, BASE, core)
+    send_offset(even, BASE, BASE, core, E_BASE)
 
     swap_x = even & (rest | ye)
 
@@ -264,39 +295,51 @@
         @pl.when(even)
         def _(i=i):
             multiply(i, SL, SM, OWN, SC)
-        send_factor(swap_x, OWN, XF, px, (i,), wait=False)
-    send_factor(swap_x, OWN, XF, px, (2,), wait=False)
+        send_factor(swap_x, OWN, XF, px, E_X, (i,))
+    send_factor(swap_x, OWN, XF, px, E_X, (2,), ends=E_X2)
+
+    early_o = odd & top & (chip == 3)
 
     @pl.when(odd)
     def _():
         fill(SL, other[...])
-        got_offsets(BASE)
-
-    early_o = odd & top & ((chip == 1) | (chip == 3))
-    fold(odd, SL, BASE, OWN, lambda s: send_offset(early_o, OWN, XO, px, (s,)))
+        fold_left(0, SL)
+        got_offset(BASE)
+        fold_right(0, SL, BASE, OWN)
+
+    send_offset(early_o, OWN, XO, px, O_X, (0, 1))
+
+    @pl.when(odd)
+    def _():
+        fold_left(1, SL)
+        fold_right(1, SL, BASE, OWN)
+
+    send_offset(early_o, OWN, XO, px, O_X, (2, 3))
 
     @pl.when(odd)
     def _():
         for i in range(2):
             multiply(i, SL, SM, None, SC)
 
-    sent_factor(swap_x, XF)
-
-    @pl.when(even & rest)
-    def _():
-        pl.semaphore_signal(turn.at[0], inc=1, device_id=(core,), device_id_type=MESH)
-
-    @pl.when(odd & rest)
-    def _():
-        pl.semaphore_wait(turn.at[0], 1)
-
-    send_offset(odd & rest, OWN, XO, px)
+    turns = rest | ye
+    wait_sent(swap_x, pm.at[OWN, :, :WIDE], E_X)
 
     @pl.when(swap_x)
     def _():
+        pl.semaphore_signal(turn, inc=1, device_id=(core,), device_id_type=MESH)
+
+    @pl.when(odd & turns)
+    def _():
+        pl.semaphore_wait(turn, 1)
+
+    send_offset(odd & turns, OWN, XO, px, O_X)
+    wait_sent(swap_x, pt.at[OWN], E_X2)
+
+    @pl.when(swap_x)
+    def _():
         got_factor(XF)
 
-    send_factor(swap_x, XF, LOW, core)
+    send_factor(swap_x, XF, LOW, core, E_LOW)
 
     @pl.when(swap_x)
     def _():
@@ -317,20 +360,23 @@
         @pl.when(swap_x)
         def _(i=i):
             multiply(i, SA, SB, PAIR, SP)
-        send_factor(swap_y, PAIR, YF, py, (i,), wait=False)
-    send_factor(swap_y, PAIR, YF, py, (2,), wait=False)
-    send_factor(swap_x & ye, PAIR, ZF, core)
-
-    o_fold = odd & (rest | (chip == 0) | (chip == 2))
-
-    @pl.when(odd & (rest | ye))
-    def _():
-        got_factor(LOW)
-        load_factor(LOW, SX)
+        send_factor(swap_y, PAIR, YF, py, E_Y, (i,))
+    send_factor(swap_y, PAIR, YF, py, E_Y, (2,), ends=E_Y2)
+    send_factor(swap_x & ye, PAIR, ZF, core, E_PAIR)
+
+    o_fold = odd & (rest | (chip < 3))
+
+    def neighbour(condition):
+        @pl.when(condition)
+        def _():
+            got_factor(LOW)
+            load_factor(LOW, SX)
+
+    neighbour(odd & turns & xl)
 
     @pl.when(o_fold)
     def _():
-        got_offsets(XO)
+        got_offset(XO)
 
     @pl.when(o_fold & xe)
     def _():
@@ -345,29 +391,31 @@
         so[BASE] = so[XO]
 
     def after_pair(s):
-        send_offset(odd & top & (chip == 2), PAIR, YO, py, (s,))
-        send_offset(odd & top & (chip == 2), PAIR, YO, me - 2, (s,), DIAG)
-        send_offset(odd & top & (chip == 0), PAIR, LOWO, px, (s,))
+        parts = (2 * s, 2 * s + 1)
+        send_offset(odd & top & (chip == 2), PAIR, YO, py, O_Y, parts)
+        send_offset(odd & top & (chip == 2), PAIR, YO, me - 2, O_TO, parts)
 
     fold(o_fold, SA, BASE, PAIR, after_pair)
-
-    sent_factor(swap_y, YF)
+    neighbour(odd & turns & xe)
+
+    wait_sent(swap_y, pm.at[PAIR, :, :WIDE], E_Y)
 
     @pl.when(swap_y)
     def _():
-        pl.semaphore_signal(turn.at[1], inc=1, device_id=(core,), device_id_type=MESH)
+        pl.semaphore_signal(turn, inc=1, device_id=(core,), device_id_type=MESH)
 
     @pl.when(odd & rest)
     def _():
-        pl.semaphore_wait(turn.at[1], 1)
-
-    send_offset(odd & rest, PAIR, YO, py)
+        pl.semaphore_wait(turn, 1)
+
+    send_offset(odd & rest, PAIR, YO, py, O_Y)
+    wait_sent(swap_y, pt.at[PAIR], E_Y2)
 
     @pl.when(swap_y)
     def _():
         got_factor(YF)
 
-    send_factor(swap_y & yl, YF, ZF, core)
+    send_factor(swap_y & yl, YF, ZF, core, E_PAIR)
 
     @pl.when(swap_y)
     def _():
@@ -379,9 +427,9 @@
         @pl.when(swap_y)
         def _(i=i):
             multiply(i, SA, SB, ALL, SR)
-        send_factor(down, ALL, ZF, me - GROUP, (i,), sem=OWN)
-    send_factor(down, ALL, ZF, me - GROUP, (2,), sem=OWN)
-    send_factor(even & chain, ALL, ALL, core)
+        send_factor(down, ALL, ZF, me - GROUP, E_ALL, (i,))
+    send_factor(down, ALL, ZF, me - GROUP, E_ALL, (2,))
+    send_factor(even & chain, ALL, ALL, core, E_ALL)
 
     @pl.when(swap_y & (chip == 0))
     def _():
@@ -411,7 +459,7 @@
         for i in range(2):
             multiply(i, SM, SB, LAST)
 
-    send_factor(hand, LAST, LAST, core)
+    send_factor(hand, LAST, LAST, core, E_LAST)
 
     z_fold = odd & (rest | ye)
 
@@ -420,13 +468,12 @@
         got_factor(ZF)
         load_factor(ZF, SP)
 
-    @pl.when(odd & top & (chip == 1))
-    def _():
-        got_offsets(LOWO)
-
     @pl.when(z_fold)
     def _():
-        got_offsets(YO)
+        got_offset(YO)
+
+    late = top | ((chip == 1) & (group == groups - 2))
+    send(odd & jnp.logical_not(late), lambda: copy(l_ref, prev, n_send, n_recv, me + 1))
 
     @pl.when(odd & rest & yl)
     def _():
@@ -437,51 +484,70 @@
     def _():
         spread(YO, to_slot(SZ))
 
-    @pl.when(odd & ye & (rest | (chip == 0)))
+    @pl.when(odd & ye)
     def _():
         so[BASE] = so[PAIR]
-
-    @pl.when(odd & top & (chip == 1))
-    def _():
-        so[BASE] = so[LOWO]
 
     far = group == 2 if joined else me < 0
     near = (group >= 2) if joined else (group >= 1)
 
     def after_all(s):
-        send_offset(odd & top & ye & near, ALL, EDGE, me - GROUP, (s,))
-        send_offset(odd & top & ye & far, ALL, EDGE, me - 2 * GROUP, (s,), ZO)
-
-    fold(z_fold, SP, BASE, ALL, after_all)
-    send_offset(odd & top & ye & near, ALL, EDGE, me - GROUP + 4, (0, 1), EDGE2)
-    send_offset(odd & top & ye & far, ALL, EDGE, me - 2 * GROUP + 4, (0, 1), DIAG)
-    send_offset(odd & rest & (group == 1) & joined, ALL, ZO, me - GROUP)
+        parts = (2 * s, 2 * s + 1)
+        send_offset(odd & top & ye & near, ALL, EDGE, me - GROUP, O_NEAR, parts)
+        send_offset(odd & top & ye & far, ALL, EDGE, me - 2 * GROUP, O_FAR, parts[1 - s:], PARTS - 1)
+
+    @pl.when(odd & rest)
+    def _():
+        fold_at_once(SP, BASE, ALL)
+
+    fold(odd & top & ye, SP, BASE, ALL, after_all)
+    send_offset(odd & top & ye & near, ALL, EDGE, me - GROUP + 4, O_NEAR2)
+    send_offset(odd & top & ye & far, ALL, EDGE, me - 2 * GROUP + 4, O_FAR2, (1, 2, 3), PARTS - 1)
+    send_offset(odd & rest & (group == 1) & joined, ALL, ZO, me - GROUP, O_Z)
 
     @pl.when(odd & chain)
     def _():
         got_factor(ALL)
         load_factor(ALL, SR)
 
+    def take_edge(condition, hand_on, relay, s):
+        for q in (2 * s, 2 * s + 1):
+            @pl.when(condition)
+            def _(q=q):
+                got_edge(q)
+
+            send_offset(hand_on, EDGE, EDGE, core, O_TO, (q,))
+            if q == 0 and relay is not None:
+                start(relay, lambda: copy(
+                    so.at[EDGE, quarter(0), :], so.at[EDGE, quarter(0), :],
+                    sent.at[O_FAR], got.at[R_OFFSET[EDGE]], me - GROUP,
+                ))
+                leave(relay, so.at[EDGE, quarter(0), :], O_FAR)
+
     for s in range(2):
-        @pl.when(odd & chain)
-        def _(s=s):
-            got_offset(EDGE, s)
-        send_offset(odd & chain, EDGE, EDGE, core, (s,), CHAIN)
+        take_edge(odd & chain, odd & chain, None, s)
 
         @pl.when(odd & chain)
         def _(s=s):
             spread(EDGE, to_slot(SZ), (s,))
 
     def after_chain(s):
-        send_offset(odd & chain & far, CHAIN, EDGE, me - 2 * GROUP, (s,), EDGE2)
-        send_offset(odd & chain & near, CHAIN, EDGE, me - GROUP, (s,))
+        to_near, to_far = odd & chain & near, odd & chain & far
+        if s == 0:
+            send_offset(to_near, CHAIN, EDGE, me - GROUP, O_NEAR, (0,))
+            send_offset(to_far, CHAIN, EDGE, me - 2 * GROUP, O_FAR, (1,))
+            send_offset(to_near & jnp.logical_not(far), CHAIN, EDGE, me - GROUP, O_NEAR, (1,))
+        else:
+            send_offset(to_far, CHAIN, EDGE, me - 2 * GROUP, O_FAR, (2, 3), PARTS - 1)
+            send_offset(to_near & far, CHAIN, EDGE, me - GROUP, O_NEAR, (1,))
+            send_offset(to_near, CHAIN, EDGE, me - GROUP, O_NEAR, (2, 3))
 
     fold(odd & chain, SR, ALL, CHAIN, after_chain)
-    send(odd & (me < n - 1), lambda: copy(l_ref, prev, n_send, n_recv, me + 1))
-
-    send_offset(odd & (chip == 0), ALL, EVEN, core)
-    send_offset(odd & (chip == 2), PAIR, EVEN, core)
-    send_offset(odd & (chip == 3), OWN, EVEN, core)
+    send(odd & late & (me < n - 1), lambda: copy(l_ref, prev, n_send, n_recv, me + 1))
+
+    send_offset(odd & (chip == 0), ALL, EVEN, core, O_EVEN)
+    send_offset(odd & (chip == 2), PAIR, EVEN, core, O_EVEN)
+    send_offset(odd & (chip == 3), OWN, EVEN, core, O_EVEN)
     low_y = odd & ye
 
     @pl.when(low_y)
@@ -498,8 +564,11 @@
         high[SA], low[SA] = high[SX], low[SX]
         so[BASE] = so[XO]
 
-    fold(low_y, SA, BASE, EVEN)
-    send_offset(odd & (chip == 1), EVEN, EVEN, core)
+    @pl.when(low_y)
+    def _():
+        fold_at_once(SA, BASE, EVEN)
+
+    send_offset(odd & (chip == 1), EVEN, EVEN, core, O_EVEN)
 
     @pl.when(odd & (chip == 0))
     def _():
@@ -532,14 +601,14 @@
 
     @pl.when(even)
     def _():
-        got_offsets(EVEN)
+        got_offset(EVEN)
         spread(EVEN, to_ref(acc))
 
     @pl.when(bottom & even)
     def _():
         got_factor(ZF)
 
-    send_factor(bottom & even, ZF, YF, core)
+    send_factor(bottom & even, ZF, YF, core, E_ALL)
 
     @pl.when(bottom & even)
     def _():
@@ -554,9 +623,9 @@
     def _():
         for i in range(2):
             multiply(i, SA, SR, None, SB)
-        got_offsets(ZO)
-
-    send_offset(bottom & odd, ZO, ZO, core)
+        got_offset(ZO)
+
+    send_offset(bottom & odd, ZO, ZO, core, O_Z)
 
     @pl.when(bottom)
     def _():
@@ -577,12 +646,14 @@
     def _():
         q_ref[...] = jnp.zeros_like(q_ref)
 
+    drain()
+
+    apart = rest & jnp.logical_not(chain)
     for s in range(2):
-        @pl.when(rest & (even | jnp.logical_not(chain)))
-        def _(s=s):
-            got_offset(EDGE, s)
-
-        send_offset(rest & odd & jnp.logical_not(chain), EDGE, EDGE, core, (s,), CHAIN)
+        take_edge(
+            rest & (even | jnp.logical_not(chain)), odd & apart,
+            odd & (group == 1) & rest if joined else None, s,
+        )
 
         @pl.when(rest)
         def _(s=s):
@@ -596,22 +667,23 @@
     def _():
         x_ref[...] = acc[...]
 
-    for condition, make in pending:
-        @pl.when(condition)
-        def _(make=make):
-            make().wait_send()
+    drain()
 
 
 def finish(x_ref, q_ref, d_any, c_any, c_ref, xh, xl, qh, ql, sem):
     d_out = pltpu.make_async_copy(x_ref, d_any, sem.at[0])
     d_out.start()
-    split(x_ref[...], xh, xl)
     split(q_ref[...], qh, ql)
-    c_ref[...] = product((xh, xl), (qh, ql), NT)
-    c_out = pltpu.make_async_copy(c_ref, c_any, sem.at[1])
-    c_out.start()
-    d_out.wait()
-    c_out.wait()
+    half = x_ref.shape[0] // 2
+    copies = [d_out]
+    for i in range(2):
+        rows = slice(i * half, (i + 1) * half)
+        split(x_ref[rows, :], xh.at[rows, :], xl.at[rows, :])
+        c_ref[rows, :] = product((xh.at[rows, :], xl.at[rows, :]), (qh, ql), NT)
+        copies.append(pltpu.make_async_copy(c_ref.at[rows, :], c_any.at[rows, :], sem.at[1 + i]))
+        copies[-1].start()
+    for c in copies:
+        c.wait()
 
 
 def local(n, schur_inverse, sweep_factor):
@@ -627,11 +699,11 @@
         scratch_shapes=[pltpu.VMEM(full, f32)] * 5 + [
             pltpu.VMEM((8,) + full, f32),
             pltpu.VMEM((8, order // 2, STRIP), f32),
-            pltpu.VMEM((11, WIDE, WIDE), f32),
+            pltpu.VMEM((10, WIDE, WIDE), f32),
             pltpu.VMEM((11,) + full, bf16),
             pltpu.VMEM((11,) + full, bf16),
-            dma((8, 3)), dma((8, 3)), dma((13, 2)), dma((13, 2)),
-            dma, dma, dma, dma, dma((2,)), pltpu.SemaphoreType.REGULAR((2,)),
+            pltpu.VMEM((order * WIDE // STRIP + order // 2, STRIP), f32),
+            dma((9,)), dma((9 + PARTS,)), dma, dma, dma, dma, dma((2,)), pltpu.SemaphoreType.REGULAR,
         ],
         compiler_params=pltpu.CompilerParams(
             collective_id=0, has_side_effects=True
@@ -642,7 +714,7 @@
         out_shape=[jax.ShapeDtypeStruct(full, f32)] * 2,
         in_specs=[pl.BlockSpec(memory_space=pltpu.VMEM)] * 2,
         out_specs=[pl.BlockSpec(memory_space=pl.ANY)] * 2,
-        scratch_shapes=[pltpu.VMEM(full, f32)] + [pltpu.VMEM(full, bf16)] * 4 + [dma((2,))],
+        scratch_shapes=[pltpu.VMEM(full, f32)] + [pltpu.VMEM(full, bf16)] * 4 + [dma((3,))],
     )(*(pltpu.with_memory_space_constraint(v, pltpu.VMEM) for v in (current, previous)))
     return diagonal[None], coupling[None]
 

time: 43.9 us -> 41.4 us (0.943)
  the two profiles are of different devices: /device:TPU:14 before, /device:TPU:0 now
where the time goes in v3:
time: 41.4 us; the launch traced here: 41.2 us
  Pallas kernels  40.4 us (98%)
  between operations  0.8 us (2%)
    pallas_call x1, Pallas kernels, local(): pl.pallas_call(functools.partial(kernel, n), out_shape=[pltpu.VMEM(full,...  39 us
    pallas_call x1, Pallas kernels, local(): pl.pallas_call(finish, out_shape=[jax.ShapeDtypeStruct(full, f32)] * 2, i...  1.42 us

profile of v3, /device:TPU:0, one launch (start us, length us, event | category | flops | bytes accessed | tf_op | source)
XLA Modules:
  0.0 41.2 jit_solution(3859013628190242736)
XLA Ops:
  0.6 39.0 %shard_map.41 = (f32[320,320]{1,0:T(8,128)S(1)}, f32[320,320]{1,0:T(8,128)S(1)}) custom-call(f32[320,320]{1,0:T(8,128)} %bitcast.4, f32[320,320]{1,0:T(8,128)} %bitcast.5), custom_call_target="tpu_custom_call" | custom-call | tf_op jit(solution)/shard_map/pallas_call | solution.py:694
  39.7 1.4 %shard_map.42 = (f32[320,320]{1,0:T(8,128)}, f32[320,320]{1,0:T(8,128)}) custom-call(f32[320,320]{1,0:T(8,128)S(1)} %get-tuple-element.6.x_ref, f32[320,320]{1,0:T(8,128)S(1)} %get-tuple-element.7.q_ref), custom_call_target="tpu_custom_call" | custom-call | tf_op jit(solution)/shard_map/pallas_call | solution.py:712

commit v4 on v3

--- a/solution.py
+++ b/solution.py
@@ -21,6 +21,7 @@
 O_X, O_Y, O_TO, O_NEAR, O_NEAR2, O_FAR, O_FAR2, O_Z, O_EVEN = range(9)
 R_FACTOR = {XF: 0, YF: 1, ZF: 2, LOW: 0, ALL: 3, LAST: 4}
 R_OFFSET = {BASE: 5, EVEN: 5, XO: 6, YO: 7, ZO: 8, EDGE: 9}
+R_ZF2 = 13
 PARTS = 4
 
 
@@ -123,36 +124,41 @@
         pending.clear()
 
     def factor(i):
-        return pm.at[i, :half, :WIDE], pm.at[i, half:, :WIDE], pt.at[i]
+        mid = half // 2
+        return pm.at[i, :half, :WIDE], pm.at[i, half:, :WIDE], pt.at[i, :mid], pt.at[i, mid:]
 
     def quarter(s, count=1):
         return slice(s * WIDE // PARTS, (s + count) * WIDE // PARTS)
 
+    half_tally = tally.at[:tally.shape[0] // 2, :]
+
     def leave(condition, ref, sem):
         pending.append((condition, lambda: copy(ref, ref, sent.at[sem], got.at[0], core)))
 
-    def send_factor(condition, src, dst, target, sem, parts=(0, 1, 2), ends=None):
+    def send_factor(condition, src, dst, target, sem, parts=(0, 1, 2, 3), ends=None, recv=None, last=3):
         for s in parts:
             start(
                 condition,
                 lambda s=s: copy(
                     factor(src)[s], factor(dst)[s],
-                    sent.at[ends if s == 2 and ends is not None else sem], got.at[R_FACTOR[dst]], target,
+                    sent.at[ends if s >= 2 and ends is not None else sem],
+                    got.at[R_FACTOR[dst] if recv is None else recv], target,
                 ),
             )
-        if 2 in parts and ends is None:
+        if last in parts and ends is None:
             leave(condition, tally, sem)
 
-    def send_offset(condition, src, dst, target, sem, parts=range(PARTS), count=PARTS):
+    def send_offset(condition, src, dst, target, sem, parts=range(PARTS), count=PARTS, recv=None, last=PARTS - 1):
         for s in parts:
             start(
                 condition,
                 lambda s=s: copy(
                     so.at[src, quarter(s), :], so.at[dst, quarter(s), :],
-                    sent.at[sem], got.at[R_OFFSET[dst] + (s if dst == EDGE else 0)], target,
+                    sent.at[sem],
+                    got.at[R_OFFSET[dst] + (s if dst == EDGE else 0) if recv is None else recv], target,
                 ),
             )
-        if PARTS - 1 in parts:
+        if last in parts:
             leave(condition, so.at[src, quarter(0, count), :], sem)
 
     def wait_sent(condition, ref, sem):
@@ -296,7 +302,7 @@
         def _(i=i):
             multiply(i, SL, SM, OWN, SC)
         send_factor(swap_x, OWN, XF, px, E_X, (i,))
-    send_factor(swap_x, OWN, XF, px, E_X, (2,), ends=E_X2)
+    send_factor(swap_x, OWN, XF, px, E_X, (2, 3), ends=E_X2)
 
     early_o = odd & top & (chip == 3)
 
@@ -333,7 +339,14 @@
         pl.semaphore_wait(turn, 1)
 
     send_offset(odd & turns, OWN, XO, px, O_X)
-    wait_sent(swap_x, pt.at[OWN], E_X2)
+
+    def send_coupling(condition):
+        send(odd & condition & (me < n - 1), lambda: copy(l_ref, prev, n_send, n_recv, me + 1))
+
+    soon = (rest & xe) | (bottom & (chip == 1)) | (top & (chip == 0))
+    late = (top & (chip > 0)) | (jnp.logical_not(bottom) & (chip == 1) & (group == groups - 2))
+    send_coupling(soon)
+    leave(swap_x, pt.at[OWN], E_X2)
 
     @pl.when(swap_x)
     def _():
@@ -356,12 +369,14 @@
 
     ordered(swap_x, xe, SC, SX, SA, SB)
     swap_y = even & rest
+    tells = rest & jnp.logical_not(bottom & (chip == 0))
+    hears = rest & jnp.logical_not(bottom & (chip == 2))
     for i in range(2):
         @pl.when(swap_x)
         def _(i=i):
             multiply(i, SA, SB, PAIR, SP)
-        send_factor(swap_y, PAIR, YF, py, E_Y, (i,))
-    send_factor(swap_y, PAIR, YF, py, E_Y, (2,), ends=E_Y2)
+        send_factor(even & tells, PAIR, YF, py, E_Y, (i,))
+    send_factor(even & tells, PAIR, YF, py, E_Y, (2, 3), ends=E_Y2)
     send_factor(swap_x & ye, PAIR, ZF, core, E_PAIR)
 
     o_fold = odd & (rest | (chip < 3))
@@ -398,7 +413,7 @@
     fold(o_fold, SA, BASE, PAIR, after_pair)
     neighbour(odd & turns & xe)
 
-    wait_sent(swap_y, pm.at[PAIR, :, :WIDE], E_Y)
+    wait_sent(even & tells, pm.at[PAIR, :, :WIDE], E_Y)
 
     @pl.when(swap_y)
     def _():
@@ -408,27 +423,29 @@
     def _():
         pl.semaphore_wait(turn, 1)
 
-    send_offset(odd & rest, PAIR, YO, py, O_Y)
-    wait_sent(swap_y, pt.at[PAIR], E_Y2)
-
-    @pl.when(swap_y)
+    send_offset(odd & tells, PAIR, YO, py, O_Y)
+    leave(even & tells, pt.at[PAIR], E_Y2)
+
+    @pl.when(even & hears)
     def _():
         got_factor(YF)
 
-    send_factor(swap_y & yl, YF, ZF, core, E_PAIR)
-
-    @pl.when(swap_y)
+    send_factor(even & hears & yl, YF, ZF, core, E_PAIR)
+
+    @pl.when(even & hears)
     def _():
         load_factor(YF, SY)
 
-    ordered(swap_y, ye, SP, SY, SA, SB)
+    ordered(even & hears, ye, SP, SY, SA, SB)
     down = even & (group == 1) & rest & joined
     for i in range(2):
-        @pl.when(swap_y)
+        @pl.when(even & hears)
         def _(i=i):
             multiply(i, SA, SB, ALL, SR)
-        send_factor(down, ALL, ZF, me - GROUP, E_ALL, (i,))
-    send_factor(down, ALL, ZF, me - GROUP, E_ALL, (2,))
+        send_factor(down & (b1 == i), ALL, ZF, me - GROUP, E_ALL, (i,))
+    for i in range(2):
+        send_factor(down & (b1 == i), ALL, ZF, me - GROUP, E_ALL, (2 + i,), last=None)
+    leave(down, half_tally, E_ALL)
     send_factor(even & chain, ALL, ALL, core, E_ALL)
 
     @pl.when(swap_y & (chip == 0))
@@ -461,7 +478,7 @@
 
     send_factor(hand, LAST, LAST, core, E_LAST)
 
-    z_fold = odd & (rest | ye)
+    z_fold = odd & (hears | (top & ye))
 
     @pl.when(z_fold)
     def _():
@@ -472,10 +489,9 @@
     def _():
         got_offset(YO)
 
-    late = top | ((chip == 1) & (group == groups - 2))
-    send(odd & jnp.logical_not(late), lambda: copy(l_ref, prev, n_send, n_recv, me + 1))
-
-    @pl.when(odd & rest & yl)
+    send_coupling(jnp.logical_not(soon | late))
+
+    @pl.when(odd & hears & yl)
     def _():
         spread(PAIR, to_slot(SZ))
         so[BASE] = so[YO]
@@ -496,7 +512,7 @@
         send_offset(odd & top & ye & near, ALL, EDGE, me - GROUP, O_NEAR, parts)
         send_offset(odd & top & ye & far, ALL, EDGE, me - 2 * GROUP, O_FAR, parts[1 - s:], PARTS - 1)
 
-    @pl.when(odd & rest)
+    @pl.when(odd & hears)
     def _():
         fold_at_once(SP, BASE, ALL)
 
@@ -510,26 +526,24 @@
         got_factor(ALL)
         load_factor(ALL, SR)
 
-    def take_edge(condition, hand_on, relay, s):
-        for q in (2 * s, 2 * s + 1):
+    def take_edge(condition, hand_on, relay, quarters):
+        for q in quarters:
             @pl.when(condition)
             def _(q=q):
                 got_edge(q)
 
-            send_offset(hand_on, EDGE, EDGE, core, O_TO, (q,))
-            if q == 0 and relay is not None:
-                start(relay, lambda: copy(
-                    so.at[EDGE, quarter(0), :], so.at[EDGE, quarter(0), :],
-                    sent.at[O_FAR], got.at[R_OFFSET[EDGE]], me - GROUP,
-                ))
-                leave(relay, so.at[EDGE, quarter(0), :], O_FAR)
+            send_offset(hand_on, EDGE, EDGE, core, O_TO, (q,), last=None)
+            if relay is not None:
+                send_offset(relay, EDGE, EDGE, me - GROUP, O_FAR, (q,), 1, last=q)
 
     for s in range(2):
-        take_edge(odd & chain, odd & chain, None, s)
+        take_edge(odd & chain, odd & chain, None, (2 * s, 2 * s + 1))
 
         @pl.when(odd & chain)
         def _(s=s):
             spread(EDGE, to_slot(SZ), (s,))
+
+    leave(odd & chain, so.at[EDGE], O_TO)
 
     def after_chain(s):
         to_near, to_far = odd & chain & near, odd & chain & far
@@ -543,7 +557,7 @@
             send_offset(to_near, CHAIN, EDGE, me - GROUP, O_NEAR, (2, 3))
 
     fold(odd & chain, SR, ALL, CHAIN, after_chain)
-    send(odd & late & (me < n - 1), lambda: copy(l_ref, prev, n_send, n_recv, me + 1))
+    send_coupling(late)
 
     send_offset(odd & (chip == 0), ALL, EVEN, core, O_EVEN)
     send_offset(odd & (chip == 2), PAIR, EVEN, core, O_EVEN)
@@ -599,6 +613,15 @@
     def _():
         high[SA], low[SA] = high[SM], low[SM]
 
+    @pl.when(bottom & even)
+    def _():
+        copy(half_tally, half_tally, sent.at[0], got.at[R_FACTOR[ZF]], me).wait_recv()
+
+    for i in range(2):
+        send_factor(bottom & even & (b1 == i), ZF, ZF, px, E_X, (i, 2 + i), recv=R_ZF2, last=None)
+        send_factor(bottom & even & (b1 == i), ZF, YF, core, E_ALL, (i, 2 + i), last=None)
+    leave(bottom & even, half_tally, E_X)
+
     @pl.when(even)
     def _():
         got_offset(EVEN)
@@ -606,9 +629,17 @@
 
     @pl.when(bottom & even)
     def _():
-        got_factor(ZF)
-
-    send_factor(bottom & even, ZF, YF, core, E_ALL)
+        copy(half_tally, half_tally, sent.at[0], got.at[R_ZF2], me).wait_recv()
+
+    for i in range(2):
+        send_factor(bottom & even & (b1 != i), ZF, YF, core, E_ALL, (i, 2 + i), last=None)
+    leave(bottom & even, tally, E_ALL)
+
+    @pl.when(bottom & odd)
+    def _():
+        got_offset(ZO)
+
+    send_offset(bottom & odd, ZO, ZO, core, O_Z)
 
     @pl.when(bottom & even)
     def _():
@@ -619,20 +650,6 @@
         got_factor(YF)
         load_factor(YF, SR)
 
-    @pl.when(bottom)
-    def _():
-        for i in range(2):
-            multiply(i, SA, SR, None, SB)
-        got_offset(ZO)
-
-    send_offset(bottom & odd, ZO, ZO, core, O_Z)
-
-    @pl.when(bottom)
-    def _():
-        spread(ZO, to_slot(SZ))
-        fold_whole(SA, acc, acc)
-        high[SA], low[SA] = high[SB], low[SB]
-
     @pl.when(odd)
     def _():
         q_ref[...] = other[...]
@@ -646,18 +663,47 @@
     def _():
         q_ref[...] = jnp.zeros_like(q_ref)
 
+    apart = odd & rest & jnp.logical_not(chain)
+    waits = rest & (even | jnp.logical_not(chain))
+    above = waits & jnp.logical_not(bottom)
+    take_edge(above, apart & jnp.logical_not(bottom), odd & rest & (group == 1) if joined else None, (0,))
     drain()
-
-    apart = rest & jnp.logical_not(chain)
-    for s in range(2):
-        take_edge(
-            rest & (even | jnp.logical_not(chain)), odd & apart,
-            odd & (group == 1) & rest if joined else None, s,
-        )
-
-        @pl.when(rest)
-        def _(s=s):
-            spread(EDGE, to_slot(SZ), (s,))
+    take_edge(above, apart & jnp.logical_not(bottom), None, (1,))
+
+    @pl.when(rest & jnp.logical_not(bottom))
+    def _():
+        spread(EDGE, to_slot(SZ), (0,))
+
+    take_edge(above, apart & jnp.logical_not(bottom), None, (2, 3))
+
+    @pl.when(rest & jnp.logical_not(bottom))
+    def _():
+        spread(EDGE, to_slot(SZ), (1,))
+
+    take_edge(bottom, apart & bottom, None, (1, 2, 3))
+
+    @pl.when(bottom)
+    def _():
+        spread(EDGE, to_slot(SZ), (1,))
+
+    take_edge(bottom, apart & bottom, None, (0,))
+    leave(apart, so.at[EDGE], O_TO)
+
+    @pl.when(bottom)
+    def _():
+        spread(EDGE, to_slot(SZ), (0,))
+        fold_left(0, SR)
+        fold_left(1, SR)
+
+    @pl.when(bottom & even)
+    def _():
+        got_offset(ZO)
+
+    @pl.when(bottom)
+    def _():
+        fold_right(0, SR, ZO, CHAIN)
+        fold_right(1, SR, ZO, CHAIN)
+        spread(CHAIN, to_slot(SZ))
 
     @pl.when(rest)
     def _():
@@ -703,7 +749,7 @@
             pltpu.VMEM((11,) + full, bf16),
             pltpu.VMEM((11,) + full, bf16),
             pltpu.VMEM((order * WIDE // STRIP + order // 2, STRIP), f32),
-            dma((9,)), dma((9 + PARTS,)), dma, dma, dma, dma, dma((2,)), pltpu.SemaphoreType.REGULAR,
+            dma((9,)), dma((10 + PARTS,)), dma, dma, dma, dma, dma((2,)), pltpu.SemaphoreType.REGULAR,
         ],
         compiler_params=pltpu.CompilerParams(
             collective_id=0, has_side_effects=True

time: 41.4 us -> 39.3 us (0.949)
  Pallas kernels: 40.4 us -> 38.3 us
    pallas_call x1, Pallas kernels: 39 us -> 36.9 us  [local(): pl.pallas_call(functools.partial(kernel, n), out_shape=[pltpu.VMEM(full,...]
where the time goes in v4:
time: 39.3 us; the launch traced here: 39.1 us
  Pallas kernels  38.3 us (97%)
  between operations  0.8 us (2%)
    pallas_call x1, Pallas kernels, local(): pl.pallas_call(functools.partial(kernel, n), out_shape=[pltpu.VMEM(full,...  36.9 us
    pallas_call x1, Pallas kernels, local(): pl.pallas_call(finish, out_shape=[jax.ShapeDtypeStruct(full, f32)] * 2, i...  1.43 us

profile of v4, /device:TPU:0, one launch (start us, length us, event | category | flops | bytes accessed | tf_op | source)
XLA Modules:
  0.0 39.1 jit_solution(14821815472076980538)
XLA Ops:
  0.6 36.9 %shard_map.41 = (f32[320,320]{1,0:T(8,128)S(1)}, f32[320,320]{1,0:T(8,128)S(1)}) custom-call(f32[320,320]{1,0:T(8,128)} %bitcast.4, f32[320,320]{1,0:T(8,128)} %bitcast.5), custom_call_target="tpu_custom_call" | custom-call | tf_op jit(solution)/shard_map/pallas_call | solution.py:740
  37.5 1.4 %shard_map.42 = (f32[320,320]{1,0:T(8,128)}, f32[320,320]{1,0:T(8,128)}) custom-call(f32[320,320]{1,0:T(8,128)S(1)} %get-tuple-element.6.x_ref, f32[320,320]{1,0:T(8,128)S(1)} %get-tuple-element.7.q_ref), custom_call_target="tpu_custom_call" | custom-call | tf_op jit(solution)/shard_map/pallas_call | solution.py:758

commit v5 on v4

--- a/solution.py
+++ b/solution.py
@@ -16,7 +16,7 @@
 
 OWN, PAIR, ALL, LAST, XF, YF, ZF, LOW = range(8)
 CHAIN, EVEN, XO, YO, EDGE, ZO, BASE = range(3, 10)
-SL, SM, SC, SX, SY, SP, SA, SB, SR, SZ, SW = range(11)
+SL, SM, SC, SX, SY, SP, SA, SB, SR, SZ, SW, SE, SV = range(13)
 E_BASE, E_X, E_X2, E_LOW, E_PAIR, E_Y, E_Y2, E_ALL, E_LAST = range(9)
 O_X, O_Y, O_TO, O_NEAR, O_NEAR2, O_FAR, O_FAR2, O_Z, O_EVEN = range(9)
 R_FACTOR = {XF: 0, YF: 1, ZF: 2, LOW: 0, ALL: 3, LAST: 4}
@@ -227,13 +227,13 @@
             ref[rows, columns] = value
         return put
 
-    def fold_left(s, k):
+    def fold_left(s, k, z=SZ, w=SW):
         a, b = ((0, STRIP), (STRIP, order))[s]
-        split(product(slot(k, a, b), slot(SZ), NN), *slot(SW, a, b))
-
-    def fold_right(s, k, base, out):
+        split(product(slot(k, a, b), slot(z), NN), *slot(w, a, b))
+
+    def fold_right(s, k, base, out, w=SW):
         a, b = ((0, STRIP), (STRIP, order))[s]
-        term = product(slot(SW, a, b), slot(k, a), NT)
+        term = product(slot(w, a, b), slot(k, a), NT)
         if s == 0:
             so[out, first, :] = so[base, first, :] + term[:, :WIDE]
             so[out, second, left] = so[base, second, left] + term[:, WIDE:]
@@ -410,8 +410,13 @@
         send_offset(odd & top & (chip == 2), PAIR, YO, py, O_Y, parts)
         send_offset(odd & top & (chip == 2), PAIR, YO, me - 2, O_TO, parts)
 
-    fold(o_fold, SA, BASE, PAIR, after_pair)
-    neighbour(odd & turns & xe)
+    stepped = odd & top & (chip == 2)
+    fold(stepped, SA, BASE, PAIR, after_pair)
+
+    @pl.when(o_fold & jnp.logical_not(stepped))
+    def _():
+        fold_at_once(SA, BASE, PAIR)
+
 
     wait_sent(even & tells, pm.at[PAIR, :, :WIDE], E_Y)
 
@@ -485,6 +490,16 @@
         got_factor(ZF)
         load_factor(ZF, SP)
 
+    sharing = groups >= 4
+    hands = odd & ye & (group == groups - 2) & sharing
+    passes = odd & top & yl & sharing
+    for q in range(PARTS // 2):
+        @pl.when(passes)
+        def _(q=q):
+            got_edge(q)
+
+        send_offset(passes, EDGE, EDGE, me - GROUP, O_NEAR, (q,), PARTS // 2, last=1)
+
     @pl.when(z_fold)
     def _():
         got_offset(YO)
@@ -506,19 +521,24 @@
 
     far = group == 2 if joined else me < 0
     near = (group >= 2) if joined else (group >= 1)
+
+    shared = (2, 3) if sharing else range(PARTS)
 
     def after_all(s):
         parts = (2 * s, 2 * s + 1)
         send_offset(odd & top & ye & near, ALL, EDGE, me - GROUP, O_NEAR, parts)
-        send_offset(odd & top & ye & far, ALL, EDGE, me - 2 * GROUP, O_FAR, parts[1 - s:], PARTS - 1)
-
-    @pl.when(odd & hears)
+        send_offset(odd & top & ye & far, ALL, EDGE, me - 2 * GROUP, O_FAR, parts)
+        if s == 0:
+            send_offset(odd & top & ye & sharing, ALL, EDGE, py, O_TO, parts, PARTS // 2, last=1)
+        else:
+            send_offset(odd & top & ye & near, ALL, EDGE, me - GROUP + 4, O_NEAR2, shared, len(shared))
+
+    @pl.when(odd & hears & jnp.logical_not(hands))
     def _():
         fold_at_once(SP, BASE, ALL)
 
     fold(odd & top & ye, SP, BASE, ALL, after_all)
-    send_offset(odd & top & ye & near, ALL, EDGE, me - GROUP + 4, O_NEAR2)
-    send_offset(odd & top & ye & far, ALL, EDGE, me - 2 * GROUP + 4, O_FAR2, (1, 2, 3), PARTS - 1)
+    send_offset(odd & top & ye & far, ALL, EDGE, me - 2 * GROUP + 4, O_FAR2)
     send_offset(odd & rest & (group == 1) & joined, ALL, ZO, me - GROUP, O_Z)
 
     @pl.when(odd & chain)
@@ -526,37 +546,51 @@
         got_factor(ALL)
         load_factor(ALL, SR)
 
-    def take_edge(condition, hand_on, relay, quarters):
+    def take_edge(condition, hand_on, quarters):
         for q in quarters:
             @pl.when(condition)
             def _(q=q):
                 got_edge(q)
 
             send_offset(hand_on, EDGE, EDGE, core, O_TO, (q,), last=None)
-            if relay is not None:
-                send_offset(relay, EDGE, EDGE, me - GROUP, O_FAR, (q,), 1, last=q)
-
+
+    alone = odd & chain & jnp.logical_not(hands)
     for s in range(2):
-        take_edge(odd & chain, odd & chain, None, (2 * s, 2 * s + 1))
+        take_edge(odd & chain, odd & chain, (2 * s, 2 * s + 1))
 
         @pl.when(odd & chain)
         def _(s=s):
-            spread(EDGE, to_slot(SZ), (s,))
+            spread(EDGE, to_slot(SE), (s,))
 
     leave(odd & chain, so.at[EDGE], O_TO)
 
-    def after_chain(s):
-        to_near, to_far = odd & chain & near, odd & chain & far
-        if s == 0:
-            send_offset(to_near, CHAIN, EDGE, me - GROUP, O_NEAR, (0,))
-            send_offset(to_far, CHAIN, EDGE, me - 2 * GROUP, O_FAR, (1,))
-            send_offset(to_near & jnp.logical_not(far), CHAIN, EDGE, me - GROUP, O_NEAR, (1,))
-        else:
-            send_offset(to_far, CHAIN, EDGE, me - 2 * GROUP, O_FAR, (2, 3), PARTS - 1)
-            send_offset(to_near & far, CHAIN, EDGE, me - GROUP, O_NEAR, (1,))
-            send_offset(to_near, CHAIN, EDGE, me - GROUP, O_NEAR, (2, 3))
-
-    fold(odd & chain, SR, ALL, CHAIN, after_chain)
+    def after_chain(condition, s):
+        to_near, to_far = condition & near, condition & far
+        parts = (2 * s, 2 * s + 1)
+        send_offset(to_far, CHAIN, EDGE, me - 2 * GROUP, O_FAR, parts)
+        send_offset(to_near & jnp.logical_not(far), CHAIN, EDGE, me - GROUP, O_NEAR, parts)
+        if s == 1:
+            send_offset(to_near & far, CHAIN, EDGE, me - GROUP, O_NEAR2)
+
+    for s in range(2):
+        @pl.when(hands)
+        def _(s=s):
+            fold_left(s, SR, SE, SV)
+            fold_left(s, SP)
+            fold_right(s, SP, BASE, ALL)
+            fold_right(s, SR, ALL, CHAIN, SV)
+
+        after_chain(hands, s)
+
+    for s in range(2):
+        @pl.when(alone)
+        def _(s=s):
+            fold_left(s, SR, SE)
+            fold_right(s, SR, ALL, CHAIN)
+
+        after_chain(alone, s)
+
+    neighbour(odd & turns & xe)
     send_coupling(late)
 
     send_offset(odd & (chip == 0), ALL, EVEN, core, O_EVEN)
@@ -635,63 +669,48 @@
         send_factor(bottom & even & (b1 != i), ZF, YF, core, E_ALL, (i, 2 + i), last=None)
     leave(bottom & even, tally, E_ALL)
 
+    @pl.when(bottom & even)
+    def _():
+        load_factor(ZF, SR)
+
+    @pl.when(odd)
+    def _():
+        q_ref[...] = other[...]
+
+    @pl.when(even & (me > 0))
+    def _():
+        copy(prev, prev, n_send, n_recv, me).wait_recv()
+        q_ref[...] = prev[...]
+
+    @pl.when(me == 0)
+    def _():
+        q_ref[...] = jnp.zeros_like(q_ref)
+
+    apart = odd & rest & jnp.logical_not(chain)
+    waits = rest & (even | jnp.logical_not(chain))
+    drain()
+    for s in range(2):
+        take_edge(waits, apart, (2 * s, 2 * s + 1))
+
+        @pl.when(rest)
+        def _(s=s):
+            spread(EDGE, to_slot(SZ), (s,))
+
+    leave(apart, so.at[EDGE], O_TO)
+
     @pl.when(bottom & odd)
     def _():
         got_offset(ZO)
 
     send_offset(bottom & odd, ZO, ZO, core, O_Z)
-
-    @pl.when(bottom & even)
-    def _():
-        load_factor(ZF, SR)
 
     @pl.when(bottom & odd)
     def _():
         got_factor(YF)
         load_factor(YF, SR)
 
-    @pl.when(odd)
-    def _():
-        q_ref[...] = other[...]
-
-    @pl.when(even & (me > 0))
-    def _():
-        copy(prev, prev, n_send, n_recv, me).wait_recv()
-        q_ref[...] = prev[...]
-
-    @pl.when(me == 0)
-    def _():
-        q_ref[...] = jnp.zeros_like(q_ref)
-
-    apart = odd & rest & jnp.logical_not(chain)
-    waits = rest & (even | jnp.logical_not(chain))
-    above = waits & jnp.logical_not(bottom)
-    take_edge(above, apart & jnp.logical_not(bottom), odd & rest & (group == 1) if joined else None, (0,))
-    drain()
-    take_edge(above, apart & jnp.logical_not(bottom), None, (1,))
-
-    @pl.when(rest & jnp.logical_not(bottom))
-    def _():
-        spread(EDGE, to_slot(SZ), (0,))
-
-    take_edge(above, apart & jnp.logical_not(bottom), None, (2, 3))
-
-    @pl.when(rest & jnp.logical_not(bottom))
-    def _():
-        spread(EDGE, to_slot(SZ), (1,))
-
-    take_edge(bottom, apart & bottom, None, (1, 2, 3))
-
     @pl.when(bottom)
     def _():
-        spread(EDGE, to_slot(SZ), (1,))
-
-    take_edge(bottom, apart & bottom, None, (0,))
-    leave(apart, so.at[EDGE], O_TO)
-
-    @pl.when(bottom)
-    def _():
-        spread(EDGE, to_slot(SZ), (0,))
         fold_left(0, SR)
         fold_left(1, SR)
 
@@ -746,8 +765,8 @@
             pltpu.VMEM((8,) + full, f32),
             pltpu.VMEM((8, order // 2, STRIP), f32),
             pltpu.VMEM((10, WIDE, WIDE), f32),
-            pltpu.VMEM((11,) + full, bf16),
-            pltpu.VMEM((11,) + full, bf16),
+            pltpu.VMEM((13,) + full, bf16),
+            pltpu.VMEM((13,) + full, bf16),
             pltpu.VMEM((order * WIDE // STRIP + order // 2, STRIP), f32),
             dma((9,)), dma((10 + PARTS,)), dma, dma, dma, dma, dma((2,)), pltpu.SemaphoreType.REGULAR,
         ],

time: 39.3 us -> 37.9 us (0.964)
  Pallas kernels: 38.3 us -> 37 us
    pallas_call x1, Pallas kernels: 36.9 us -> 35.6 us  [local(): pl.pallas_call(functools.partial(kernel, n), out_shape=[pltpu.VMEM(full,...]
where the time goes in v5:
time: 37.9 us; the launch traced here: 37.8 us
  Pallas kernels  37 us (98%)
  between operations  0.8 us (2%)
    pallas_call x1, Pallas kernels, local(): pl.pallas_call(functools.partial(kernel, n), out_shape=[pltpu.VMEM(full,...  35.6 us
    pallas_call x1, Pallas kernels, local(): pl.pallas_call(finish, out_shape=[jax.ShapeDtypeStruct(full, f32)] * 2, i...  1.42 us

profile of v5, /device:TPU:0, one launch (start us, length us, event | category | flops | bytes accessed | tf_op | source)
XLA Modules:
  0.0 37.8 jit_solution(1328050078561201816)
XLA Ops:
  0.6 35.6 %shard_map.41 = (f32[320,320]{1,0:T(8,128)S(1)}, f32[320,320]{1,0:T(8,128)S(1)}) custom-call(f32[320,320]{1,0:T(8,128)} %bitcast.4, f32[320,320]{1,0:T(8,128)} %bitcast.5), custom_call_target="tpu_custom_call" | custom-call | tf_op jit(solution)/shard_map/pallas_call | solution.py:759
  36.2 1.4 %shard_map.42 = (f32[320,320]{1,0:T(8,128)}, f32[320,320]{1,0:T(8,128)}) custom-call(f32[320,320]{1,0:T(8,128)S(1)} %get-tuple-element.6.x_ref, f32[320,320]{1,0:T(8,128)S(1)} %get-tuple-element.7.q_ref), custom_call_target="tpu_custom_call" | custom-call | tf_op jit(solution)/shard_map/pallas_call | solution.py:777

commit v6 on v5

--- a/solution.py
+++ b/solution.py
@@ -21,7 +21,7 @@
 O_X, O_Y, O_TO, O_NEAR, O_NEAR2, O_FAR, O_FAR2, O_Z, O_EVEN = range(9)
 R_FACTOR = {XF: 0, YF: 1, ZF: 2, LOW: 0, ALL: 3, LAST: 4}
 R_OFFSET = {BASE: 5, EVEN: 5, XO: 6, YO: 7, ZO: 8, EDGE: 9}
-R_ZF2 = 13
+R_ZF2, R_ENDS, R_ZO = 13, 14, (8, 15)
 PARTS = 4
 
 
@@ -43,7 +43,7 @@
     ) + dot(lh[...], rh[...], dims)
 
 
-def kernel(n, g_any, l_any, x_ref, q_ref, *scratch):
+def kernel(n, g_any, l_any, x_ref, xh_ref, xl_ref, qh_ref, ql_ref, *scratch):
     (g_ref, l_ref, other, prev, acc, pm, pt, so, high, low, tally,
      sent, got, l_send, l_recv, n_send, n_recv, in_sem, turn) = scratch
     order = g_ref.shape[0]
@@ -132,8 +132,12 @@
 
     half_tally = tally.at[:tally.shape[0] // 2, :]
 
-    def leave(condition, ref, sem):
-        pending.append((condition, lambda: copy(ref, ref, sent.at[sem], got.at[0], core)))
+    def leave(condition, make_ref, sem):
+        def make():
+            ref = make_ref()
+            return copy(ref, ref, sent.at[sem], got.at[0], core)
+
+        pending.append((condition, make))
 
     def send_factor(condition, src, dst, target, sem, parts=(0, 1, 2, 3), ends=None, recv=None, last=3):
         for s in parts:
@@ -146,7 +150,7 @@
                 ),
             )
         if last in parts and ends is None:
-            leave(condition, tally, sem)
+            leave(condition, lambda: tally, sem)
 
     def send_offset(condition, src, dst, target, sem, parts=range(PARTS), count=PARTS, recv=None, last=PARTS - 1):
         for s in parts:
@@ -159,7 +163,7 @@
                 ),
             )
         if last in parts:
-            leave(condition, so.at[src, quarter(0, count), :], sem)
+            leave(condition, lambda: so.at[src, quarter(0, count), :], sem)
 
     def wait_sent(condition, ref, sem):
         @pl.when(condition)
@@ -258,11 +262,14 @@
         fold_right(0, k, base, out)
         fold_right(1, k, base, out)
 
-    def fold_whole(k, base, out):
+    def fold_whole(k, base, out, parts=None):
         for a in (0, half):
             split(product(slot(k, a, a + half), slot(SZ), NN), *slot(SW, a, a + half))
         for a in (0, half):
-            out[a:a + half, :] = base[a:a + half, :] + product(slot(SW, a, a + half), slot(k), NT)
+            value = base[a:a + half, :] + product(slot(SW, a, a + half), slot(k), NT)
+            out[a:a + half, :] = value
+            if parts is not None:
+                split(value, parts[0].at[a:a + half, :], parts[1].at[a:a + half, :])
 
     l_in.wait()
 
@@ -346,7 +353,7 @@
     soon = (rest & xe) | (bottom & (chip == 1)) | (top & (chip == 0))
     late = (top & (chip > 0)) | (jnp.logical_not(bottom) & (chip == 1) & (group == groups - 2))
     send_coupling(soon)
-    leave(swap_x, pt.at[OWN], E_X2)
+    leave(swap_x, lambda: pt.at[OWN], E_X2)
 
     @pl.when(swap_x)
     def _():
@@ -396,27 +403,29 @@
     @pl.when(o_fold & xe)
     def _():
         spread(XO, to_slot(SZ))
-        high[SA], low[SA] = high[SC], low[SC]
-        so[BASE] = so[OWN]
 
     @pl.when(o_fold & xl)
     def _():
         spread(OWN, to_slot(SZ))
-        high[SA], low[SA] = high[SX], low[SX]
-        so[BASE] = so[XO]
+
+    stepped = odd & top & (chip == 2)
 
     def after_pair(s):
         parts = (2 * s, 2 * s + 1)
-        send_offset(odd & top & (chip == 2), PAIR, YO, py, O_Y, parts)
-        send_offset(odd & top & (chip == 2), PAIR, YO, me - 2, O_TO, parts)
-
-    stepped = odd & top & (chip == 2)
-    fold(stepped, SA, BASE, PAIR, after_pair)
-
-    @pl.when(o_fold & jnp.logical_not(stepped))
-    def _():
-        fold_at_once(SA, BASE, PAIR)
-
+        send_offset(stepped, PAIR, YO, py, O_Y, parts)
+        send_offset(stepped, PAIR, YO, me - 2, O_TO, parts)
+
+    @pl.when(stepped)
+    def _():
+        fold(stepped, SC, OWN, PAIR, after_pair)
+
+    @pl.when(o_fold & xe & jnp.logical_not(stepped))
+    def _():
+        fold_at_once(SC, OWN, PAIR)
+
+    @pl.when(o_fold & xl)
+    def _():
+        fold_at_once(SX, XO, PAIR)
 
     wait_sent(even & tells, pm.at[PAIR, :, :WIDE], E_Y)
 
@@ -429,59 +438,64 @@
         pl.semaphore_wait(turn, 1)
 
     send_offset(odd & tells, PAIR, YO, py, O_Y)
-    leave(even & tells, pt.at[PAIR], E_Y2)
-
-    @pl.when(even & hears)
-    def _():
-        got_factor(YF)
-
-    send_factor(even & hears & yl, YF, ZF, core, E_PAIR)
-
-    @pl.when(even & hears)
-    def _():
-        load_factor(YF, SY)
-
-    ordered(even & hears, ye, SP, SY, SA, SB)
+    leave(even & tells, lambda: pt.at[PAIR], E_Y2)
+    hears_late = even & hears & yl
     down = even & (group == 1) & rest & joined
-    for i in range(2):
+    even_chain = even & chain
+    hand = swap_y & (chip < 3)
+
+    @pl.when(even)
+    def _():
+
         @pl.when(even & hears)
-        def _(i=i):
-            multiply(i, SA, SB, ALL, SR)
-        send_factor(down & (b1 == i), ALL, ZF, me - GROUP, E_ALL, (i,))
-    for i in range(2):
-        send_factor(down & (b1 == i), ALL, ZF, me - GROUP, E_ALL, (2 + i,), last=None)
-    leave(down, half_tally, E_ALL)
-    send_factor(even & chain, ALL, ALL, core, E_ALL)
-
-    @pl.when(swap_y & (chip == 0))
-    def _():
+        def _():
+            got_factor(YF)
+
+        send_factor(hears_late, YF, ZF, core, E_PAIR)
+
+        @pl.when(even & hears)
+        def _():
+            load_factor(YF, SY)
+
+        ordered(even & hears, ye, SP, SY, SA, SB)
         for i in range(2):
-            multiply(i, SX, SY, None, SB)
-        high[SA], low[SA] = high[SR], low[SR]
-
-    @pl.when(swap_y & (chip == 1))
-    def _():
+            @pl.when(even & hears)
+            def _(i=i):
+                multiply(i, SA, SB, ALL, SR)
+            send_factor(down & (b1 == i), ALL, ZF, me - GROUP, E_ALL, (i,))
         for i in range(2):
-            multiply(i, SC, SY, None, SA)
-        high[SB], low[SB] = high[SY], low[SY]
-
-    @pl.when(swap_y & (chip == 2))
-    def _():
-        high[SA], low[SA] = high[SP], low[SP]
-        high[SB], low[SB] = high[SX], low[SX]
-
-    @pl.when(swap_y & (chip == 3))
-    def _():
-        high[SA], low[SA] = high[SC], low[SC]
-
-    hand = swap_y & (chip < 3)
-
-    @pl.when(hand)
-    def _():
-        for i in range(2):
-            multiply(i, SM, SB, LAST)
-
-    send_factor(hand, LAST, LAST, core, E_LAST)
+            send_factor(down & (b1 == i), ALL, ZF, me - GROUP, E_ALL, (2 + i,), recv=R_ENDS, last=None)
+        leave(down, lambda: half_tally, E_ALL)
+        send_factor(even_chain, ALL, ALL, core, E_ALL)
+
+        @pl.when(swap_y & (chip == 0))
+        def _():
+            for i in range(2):
+                multiply(i, SX, SY, None, SB)
+            high[SA], low[SA] = high[SR], low[SR]
+
+        @pl.when(swap_y & (chip == 1))
+        def _():
+            for i in range(2):
+                multiply(i, SC, SY, None, SA)
+            high[SB], low[SB] = high[SY], low[SY]
+
+        @pl.when(swap_y & (chip == 2))
+        def _():
+            high[SA], low[SA] = high[SP], low[SP]
+            high[SB], low[SB] = high[SX], low[SX]
+
+        @pl.when(swap_y & (chip == 3))
+        def _():
+            high[SA], low[SA] = high[SC], low[SC]
+
+
+        @pl.when(hand)
+        def _():
+            for i in range(2):
+                multiply(i, SM, SB, LAST)
+
+        send_factor(hand, LAST, LAST, core, E_LAST)
 
     z_fold = odd & (hears | (top & ye))
 
@@ -493,58 +507,14 @@
     sharing = groups >= 4
     hands = odd & ye & (group == groups - 2) & sharing
     passes = odd & top & yl & sharing
-    for q in range(PARTS // 2):
-        @pl.when(passes)
-        def _(q=q):
-            got_edge(q)
-
-        send_offset(passes, EDGE, EDGE, me - GROUP, O_NEAR, (q,), PARTS // 2, last=1)
-
-    @pl.when(z_fold)
-    def _():
-        got_offset(YO)
-
-    send_coupling(jnp.logical_not(soon | late))
-
-    @pl.when(odd & hears & yl)
-    def _():
-        spread(PAIR, to_slot(SZ))
-        so[BASE] = so[YO]
-
-    @pl.when(z_fold & ye)
-    def _():
-        spread(YO, to_slot(SZ))
-
-    @pl.when(odd & ye)
-    def _():
-        so[BASE] = so[PAIR]
-
-    far = group == 2 if joined else me < 0
-    near = (group >= 2) if joined else (group >= 1)
-
-    shared = (2, 3) if sharing else range(PARTS)
-
-    def after_all(s):
-        parts = (2 * s, 2 * s + 1)
-        send_offset(odd & top & ye & near, ALL, EDGE, me - GROUP, O_NEAR, parts)
-        send_offset(odd & top & ye & far, ALL, EDGE, me - 2 * GROUP, O_FAR, parts)
-        if s == 0:
-            send_offset(odd & top & ye & sharing, ALL, EDGE, py, O_TO, parts, PARTS // 2, last=1)
-        else:
-            send_offset(odd & top & ye & near, ALL, EDGE, me - GROUP + 4, O_NEAR2, shared, len(shared))
-
-    @pl.when(odd & hears & jnp.logical_not(hands))
-    def _():
-        fold_at_once(SP, BASE, ALL)
-
-    fold(odd & top & ye, SP, BASE, ALL, after_all)
-    send_offset(odd & top & ye & far, ALL, EDGE, me - 2 * GROUP + 4, O_FAR2)
-    send_offset(odd & rest & (group == 1) & joined, ALL, ZO, me - GROUP, O_Z)
-
-    @pl.when(odd & chain)
-    def _():
-        got_factor(ALL)
-        load_factor(ALL, SR)
+    @pl.when(passes)
+    def _():
+        for q in range(PARTS // 2):
+            @pl.when(passes)
+            def _(q=q):
+                got_edge(q)
+
+            send_offset(passes, EDGE, EDGE, me - GROUP, O_NEAR, (q,), PARTS // 2, last=1)
 
     def take_edge(condition, hand_on, quarters):
         for q in quarters:
@@ -554,41 +524,122 @@
 
             send_offset(hand_on, EDGE, EDGE, core, O_TO, (q,), last=None)
 
+    take_edge(hands, hands, (0, 1))
+
+    @pl.when(hands)
+    def _():
+        spread(EDGE, to_slot(SE), (0,))
+
+    @pl.when(z_fold)
+    def _():
+        got_offset(YO)
+
+    send_coupling(jnp.logical_not(soon | late))
+
+    @pl.when(odd & hears & yl)
+    def _():
+        spread(PAIR, to_slot(SZ))
+
+    @pl.when(z_fold & ye)
+    def _():
+        spread(YO, to_slot(SZ))
+
+    far = group == 2 if joined else me < 0
+    near = (group >= 2) if joined else (group >= 1)
+
+    shared = (2, 3) if sharing else range(PARTS)
+    heads = odd & top & ye
+    heads_near, heads_far, heads_share = heads & near, heads & far, heads & sharing
+
+    def after_all(s):
+        parts = (2 * s, 2 * s + 1)
+        send_offset(heads_near, ALL, EDGE, me - GROUP, O_NEAR, parts)
+        send_offset(heads_far, ALL, EDGE, me - 2 * GROUP, O_FAR, parts)
+        if s == 0:
+            send_offset(heads_share, ALL, EDGE, py, O_TO, parts, PARTS // 2, last=1)
+        else:
+            send_offset(heads_near, ALL, EDGE, me - GROUP + 4, O_NEAR2, shared, len(shared))
+
+    gives = odd & rest & (group == 1) & joined
+
+    @pl.when(odd & hears & ye & jnp.logical_not(hands | gives))
+    def _():
+        fold_at_once(SP, PAIR, ALL)
+
+    @pl.when(odd & hears & yl & jnp.logical_not(gives))
+    def _():
+        fold_at_once(SP, YO, ALL)
+
+    def after_given(s):
+        send_offset(gives, ALL, ZO, me - GROUP, O_Z, (2 * s, 2 * s + 1), recv=R_ZO[s])
+
+    @pl.when(gives)
+    def _():
+        @pl.when(gives & ye)
+        def _():
+            so[BASE] = so[PAIR]
+
+        @pl.when(gives & yl)
+        def _():
+            so[BASE] = so[YO]
+
+        fold(gives & jnp.logical_not(hands), SP, BASE, ALL, after_given)
+
+    @pl.when(heads)
+    def _():
+        fold(heads, SP, PAIR, ALL, after_all)
+        send_offset(heads_far, ALL, EDGE, me - 2 * GROUP + 4, O_FAR2)
+
+    @pl.when(odd & chain)
+    def _():
+        got_factor(ALL)
+        load_factor(ALL, SR)
+
     alone = odd & chain & jnp.logical_not(hands)
     for s in range(2):
-        take_edge(odd & chain, odd & chain, (2 * s, 2 * s + 1))
-
-        @pl.when(odd & chain)
+        taken = alone if s == 0 else odd & chain
+        take_edge(taken, taken, (2 * s, 2 * s + 1))
+
+        @pl.when(taken)
         def _(s=s):
             spread(EDGE, to_slot(SE), (s,))
 
-    leave(odd & chain, so.at[EDGE], O_TO)
-
-    def after_chain(condition, s):
-        to_near, to_far = condition & near, condition & far
+    leave(odd & chain, lambda: so.at[EDGE], O_TO)
+
+    routes = {
+        who: (condition & near & jnp.logical_not(far), condition & near & far, condition & far)
+        for who, condition in (("hands", hands), ("alone", alone))
+    }
+
+    def after_chain(who, s):
         parts = (2 * s, 2 * s + 1)
+        only, also, to_far = routes[who]
         send_offset(to_far, CHAIN, EDGE, me - 2 * GROUP, O_FAR, parts)
-        send_offset(to_near & jnp.logical_not(far), CHAIN, EDGE, me - GROUP, O_NEAR, parts)
+        send_offset(only, CHAIN, EDGE, me - GROUP, O_NEAR, parts)
         if s == 1:
-            send_offset(to_near & far, CHAIN, EDGE, me - GROUP, O_NEAR2)
-
-    for s in range(2):
-        @pl.when(hands)
-        def _(s=s):
-            fold_left(s, SR, SE, SV)
-            fold_left(s, SP)
-            fold_right(s, SP, BASE, ALL)
-            fold_right(s, SR, ALL, CHAIN, SV)
-
-        after_chain(hands, s)
-
-    for s in range(2):
-        @pl.when(alone)
-        def _(s=s):
-            fold_left(s, SR, SE)
-            fold_right(s, SR, ALL, CHAIN)
-
-        after_chain(alone, s)
+            send_offset(also, CHAIN, EDGE, me - GROUP, O_NEAR2)
+
+    @pl.when(hands)
+    def _():
+        for s in range(2):
+            @pl.when(hands)
+            def _(s=s):
+                fold_left(s, SR, SE, SV)
+                fold_left(s, SP)
+                fold_right(s, SP, PAIR, ALL)
+                fold_right(s, SR, ALL, CHAIN, SV)
+
+            after_chain("hands", s)
+
+    @pl.when(alone)
+    def _():
+        for s in range(2):
+            @pl.when(alone)
+            def _(s=s):
+                fold_left(s, SR, SE)
+                fold_right(s, SR, ALL, CHAIN)
+
+            after_chain("alone", s)
 
     neighbour(odd & turns & xe)
     send_coupling(late)
@@ -647,14 +698,15 @@
     def _():
         high[SA], low[SA] = high[SM], low[SM]
 
-    @pl.when(bottom & even)
-    def _():
-        copy(half_tally, half_tally, sent.at[0], got.at[R_FACTOR[ZF]], me).wait_recv()
-
-    for i in range(2):
-        send_factor(bottom & even & (b1 == i), ZF, ZF, px, E_X, (i, 2 + i), recv=R_ZF2, last=None)
-        send_factor(bottom & even & (b1 == i), ZF, YF, core, E_ALL, (i, 2 + i), last=None)
-    leave(bottom & even, half_tally, E_X)
+    for part, recv in ((0, R_FACTOR[ZF]), (2, R_ENDS)):
+        @pl.when(bottom & even)
+        def _(part=part, recv=recv):
+            ref = factor(ZF)[part]
+            copy(ref, ref, sent.at[0], got.at[recv], me).wait_recv()
+
+        for i in range(2):
+            send_factor(bottom & even & (b1 == i), ZF, ZF, px, E_X, (part + i,), recv=R_ZF2, last=None)
+            send_factor(bottom & even & (b1 == i), ZF, YF, core, E_ALL, (part + i,), last=None)
 
     @pl.when(even)
     def _():
@@ -667,7 +719,6 @@
 
     for i in range(2):
         send_factor(bottom & even & (b1 != i), ZF, YF, core, E_ALL, (i, 2 + i), last=None)
-    leave(bottom & even, tally, E_ALL)
 
     @pl.when(bottom & even)
     def _():
@@ -675,16 +726,17 @@
 
     @pl.when(odd)
     def _():
-        q_ref[...] = other[...]
+        split(other[...], qh_ref, ql_ref)
 
     @pl.when(even & (me > 0))
     def _():
         copy(prev, prev, n_send, n_recv, me).wait_recv()
-        q_ref[...] = prev[...]
+        split(prev[...], qh_ref, ql_ref)
 
     @pl.when(me == 0)
     def _():
-        q_ref[...] = jnp.zeros_like(q_ref)
+        qh_ref[...] = jnp.zeros_like(qh_ref)
+        ql_ref[...] = jnp.zeros_like(ql_ref)
 
     apart = odd & rest & jnp.logical_not(chain)
     waits = rest & (even | jnp.logical_not(chain))
@@ -696,13 +748,21 @@
         def _(s=s):
             spread(EDGE, to_slot(SZ), (s,))
 
-    leave(apart, so.at[EDGE], O_TO)
-
-    @pl.when(bottom & odd)
-    def _():
-        got_offset(ZO)
-
-    send_offset(bottom & odd, ZO, ZO, core, O_Z)
+    leave(apart, lambda: so.at[EDGE], O_TO)
+
+    def got_given(s):
+        ref = so.at[ZO, quarter(2 * s, 2), :]
+        copy(ref, ref, sent.at[0], got.at[R_ZO[s]], me).wait_recv()
+
+    for s in range(2):
+        @pl.when(bottom & odd)
+        def _(s=s):
+            got_given(s)
+
+        send_offset(bottom & odd, ZO, ZO, core, O_Z, (2 * s, 2 * s + 1), recv=R_ZO[s])
+
+    leave(bottom & even, lambda: half_tally, E_X)
+    leave(bottom & even, lambda: tally, E_ALL)
 
     @pl.when(bottom & odd)
     def _():
@@ -716,7 +776,8 @@
 
     @pl.when(bottom & even)
     def _():
-        got_offset(ZO)
+        got_given(0)
+        got_given(1)
 
     @pl.when(bottom)
     def _():
@@ -726,24 +787,22 @@
 
     @pl.when(rest)
     def _():
-        fold_whole(SA, acc, x_ref)
+        fold_whole(SA, acc, x_ref, (xh_ref, xl_ref))
 
     @pl.when(top)
     def _():
         x_ref[...] = acc[...]
+        split(acc[...], xh_ref, xl_ref)
 
     drain()
 
 
-def finish(x_ref, q_ref, d_any, c_any, c_ref, xh, xl, qh, ql, sem):
-    d_out = pltpu.make_async_copy(x_ref, d_any, sem.at[0])
-    d_out.start()
-    split(q_ref[...], qh, ql)
+def finish(x_ref, xh, xl, qh, ql, d_any, c_any, c_ref, sem):
+    copies = [pltpu.make_async_copy(x_ref, d_any, sem.at[0])]
+    copies[0].start()
     half = x_ref.shape[0] // 2
-    copies = [d_out]
     for i in range(2):
         rows = slice(i * half, (i + 1) * half)
-        split(x_ref[rows, :], xh.at[rows, :], xl.at[rows, :])
         c_ref[rows, :] = product((xh.at[rows, :], xl.at[rows, :]), (qh, ql), NT)
         copies.append(pltpu.make_async_copy(c_ref.at[rows, :], c_any.at[rows, :], sem.at[1 + i]))
         copies[-1].start()
@@ -756,11 +815,11 @@
     full = (order, order)
     f32, bf16 = jnp.float32, jnp.bfloat16
     dma = pltpu.SemaphoreType.DMA
-    current, previous = pl.pallas_call(
+    values = pl.pallas_call(
         functools.partial(kernel, n),
-        out_shape=[pltpu.VMEM(full, f32)] * 2,
+        out_shape=[pltpu.VMEM(full, f32)] + [pltpu.VMEM(full, bf16)] * 4,
         in_specs=[pl.BlockSpec(memory_space=pl.ANY)] * 2,
-        out_specs=[pl.BlockSpec(memory_space=pltpu.VMEM)] * 2,
+        out_specs=[pl.BlockSpec(memory_space=pltpu.VMEM)] * 5,
         scratch_shapes=[pltpu.VMEM(full, f32)] * 5 + [
             pltpu.VMEM((8,) + full, f32),
             pltpu.VMEM((8, order // 2, STRIP), f32),
@@ -768,7 +827,7 @@
             pltpu.VMEM((13,) + full, bf16),
             pltpu.VMEM((13,) + full, bf16),
             pltpu.VMEM((order * WIDE // STRIP + order // 2, STRIP), f32),
-            dma((9,)), dma((10 + PARTS,)), dma, dma, dma, dma, dma((2,)), pltpu.SemaphoreType.REGULAR,
+            dma((9,)), dma((12 + PARTS,)), dma, dma, dma, dma, dma((2,)), pltpu.SemaphoreType.REGULAR,
         ],
         compiler_params=pltpu.CompilerParams(
             collective_id=0, has_side_effects=True
@@ -777,10 +836,10 @@
     diagonal, coupling = pl.pallas_call(
         finish,
         out_shape=[jax.ShapeDtypeStruct(full, f32)] * 2,
-        in_specs=[pl.BlockSpec(memory_space=pltpu.VMEM)] * 2,
+        in_specs=[pl.BlockSpec(memory_space=pltpu.VMEM)] * 5,
         out_specs=[pl.BlockSpec(memory_space=pl.ANY)] * 2,
-        scratch_shapes=[pltpu.VMEM(full, f32)] + [pltpu.VMEM(full, bf16)] * 4 + [dma((3,))],
-    )(*(pltpu.with_memory_space_constraint(v, pltpu.VMEM) for v in (current, previous)))
+        scratch_shapes=[pltpu.VMEM(full, f32), dma((3,))],
+    )(*(pltpu.with_memory_space_constraint(v, pltpu.VMEM) for v in values))
     return diagonal[None], coupling[None]
 
 

time: 37.9 us -> 37.6 us (level)
  no operation moved by 1% of the time
where the time goes in v6:
time: 37.6 us; the launch traced here: 37.5 us
  Pallas kernels  36.7 us (98%)
  between operations  0.8 us (2%)
    pallas_call x1, Pallas kernels, local(): pl.pallas_call(functools.partial(kernel, n), out_shape=[pltpu.VMEM(full,...  35.3 us
    pallas_call x1, Pallas kernels, local(): pl.pallas_call(finish, out_shape=[jax.ShapeDtypeStruct(full, f32)] * 2, i...  1.42 us

profile of v6, /device:TPU:0, one launch (start us, length us, event | category | flops | bytes accessed | tf_op | source)
XLA Modules:
  0.0 37.5 jit_solution(16826709395805717924)
XLA Ops:
  0.6 35.3 %shard_map.41 = (f32[320,320]{1,0:T(8,128)S(1)}, bf16[320,320]{1,0:T(8,128)(2,1)S(1)}, bf16[320,320]{1,0:T(8,128)(2,1)S(1)}, bf16[320,320]{1,0:T(8,128)(2,1)S(1)}, bf16[320,320]{1,0:T(8,128)(2,1)S(1)}) custom-call(f32[320,320]{1,0:T(8,128)} %bitcast.4, f32[320,320]{1,0:T(8,128)} %bitcast.5), custom_call_target="tpu_custom_call" | custom-call | tf_op jit(solution)/shard_map/pallas_call | solution.py:818
  35.9 1.4 %shard_map.42 = (f32[320,320]{1,0:T(8,128)}, f32[320,320]{1,0:T(8,128)}) custom-call(f32[320,320]{1,0:T(8,128)S(1)} %get-tuple-element.9.x_ref, bf16[320,320]{1,0:T(8,128)(2,1)S(1)} %get-tuple-element.10.xh, bf16[320,320]{1,0:T(8,128)(2,1)S(1)} %get-tuple-element.11.xl, bf16[320,320]{1,0:T(8,128)(2,1)S(1)} %get-tuple-element.12.qh, ...), custom_call_target="tpu_custom_call" | custom-call | tf_op jit(solution)/shard_map/pallas_call | solution.py:836

commit v7 on v6

--- a/solution.py
+++ b/solution.py
@@ -125,7 +125,7 @@
 
     def factor(i):
         mid = half // 2
-        return pm.at[i, :half, :WIDE], pm.at[i, half:, :WIDE], pt.at[i, :mid], pt.at[i, mid:]
+        return tuple(pm.at[i, a:a + mid, :WIDE] for a in range(0, order, mid)) + (pt.at[i, :mid], pt.at[i, mid:])
 
     def quarter(s, count=1):
         return slice(s * WIDE // PARTS, (s + count) * WIDE // PARTS)
@@ -139,13 +139,13 @@
 
         pending.append((condition, make))
 
-    def send_factor(condition, src, dst, target, sem, parts=(0, 1, 2, 3), ends=None, recv=None, last=3):
+    def send_factor(condition, src, dst, target, sem, parts=range(6), ends=None, recv=None, last=5):
         for s in parts:
             start(
                 condition,
                 lambda s=s: copy(
                     factor(src)[s], factor(dst)[s],
-                    sent.at[ends if s >= 2 and ends is not None else sem],
+                    sent.at[ends if s >= 4 and ends is not None else sem],
                     got.at[R_FACTOR[dst] if recv is None else recv], target,
                 ),
             )
@@ -187,14 +187,16 @@
         split(ends[:, :tail], h.at[:half, third], l.at[:half, third])
         split(ends[:, tail:2 * tail], h.at[half:, third], l.at[half:, third])
 
-    def multiply(i, k, r, out, into=None):
-        rows = slice(i * half, (i + 1) * half)
-        value = product(slot(k, rows.start, rows.stop), slot(r), NN)
+    def multiply(a, b, k, r, out, into=None):
+        value = product(slot(k, a, b), slot(r), NN)
         if out is not None:
-            pm[out, rows, :WIDE] = value[:, :WIDE]
-            pt[out, :, i * tail:(i + 1) * tail] = value[:, third]
+            pm[out, a:b, :WIDE] = value[:, :WIDE]
+            side, low_row = a // half, a // half * half
+            pt[out, a - low_row:b - low_row, side * tail:(side + 1) * tail] = value[:, third]
         if into is not None:
-            split(value, *slot(into, rows.start, rows.stop))
+            split(value, *slot(into, a, b))
+
+    pieces = ((0, half // 2, (0,)), (half // 2, half, (1,)), (half, order, (2, 3)))
 
     def pack(ref, i):
         so[i, first, :] = ref[first, :WIDE]
@@ -304,12 +306,12 @@
     def _():
         fill(SM, other[...])
 
-    for i in range(2):
+    for a, b, parts in pieces:
         @pl.when(even)
-        def _(i=i):
-            multiply(i, SL, SM, OWN, SC)
-        send_factor(swap_x, OWN, XF, px, E_X, (i,))
-    send_factor(swap_x, OWN, XF, px, E_X, (2, 3), ends=E_X2)
+        def _(a=a, b=b):
+            multiply(a, b, SL, SM, OWN, SC)
+        send_factor(swap_x, OWN, XF, px, E_X, parts)
+    send_factor(swap_x, OWN, XF, px, E_X, (4, 5), ends=E_X2)
 
     early_o = odd & top & (chip == 3)
 
@@ -332,7 +334,7 @@
     @pl.when(odd)
     def _():
         for i in range(2):
-            multiply(i, SL, SM, None, SC)
+            multiply(i * half, (i + 1) * half, SL, SM, None, SC)
 
     turns = rest | ye
     wait_sent(swap_x, pm.at[OWN, :, :WIDE], E_X)
@@ -378,12 +380,12 @@
     swap_y = even & rest
     tells = rest & jnp.logical_not(bottom & (chip == 0))
     hears = rest & jnp.logical_not(bottom & (chip == 2))
-    for i in range(2):
+    for a, b, parts in pieces:
         @pl.when(swap_x)
-        def _(i=i):
-            multiply(i, SA, SB, PAIR, SP)
-        send_factor(even & tells, PAIR, YF, py, E_Y, (i,))
-    send_factor(even & tells, PAIR, YF, py, E_Y, (2, 3), ends=E_Y2)
+        def _(a=a, b=b):
+            multiply(a, b, SA, SB, PAIR, SP)
+        send_factor(even & tells, PAIR, YF, py, E_Y, parts)
+    send_factor(even & tells, PAIR, YF, py, E_Y, (4, 5), ends=E_Y2)
     send_factor(swap_x & ye, PAIR, ZF, core, E_PAIR)
 
     o_fold = odd & (rest | (chip < 3))
@@ -461,23 +463,23 @@
         for i in range(2):
             @pl.when(even & hears)
             def _(i=i):
-                multiply(i, SA, SB, ALL, SR)
-            send_factor(down & (b1 == i), ALL, ZF, me - GROUP, E_ALL, (i,))
+                multiply(i * half, (i + 1) * half, SA, SB, ALL, SR)
+            send_factor(down & (b1 == i), ALL, ZF, me - GROUP, E_ALL, (2 * i, 2 * i + 1))
         for i in range(2):
-            send_factor(down & (b1 == i), ALL, ZF, me - GROUP, E_ALL, (2 + i,), recv=R_ENDS, last=None)
+            send_factor(down & (b1 == i), ALL, ZF, me - GROUP, E_ALL, (4 + i,), recv=R_ENDS, last=None)
         leave(down, lambda: half_tally, E_ALL)
         send_factor(even_chain, ALL, ALL, core, E_ALL)
 
         @pl.when(swap_y & (chip == 0))
         def _():
             for i in range(2):
-                multiply(i, SX, SY, None, SB)
+                multiply(i * half, (i + 1) * half, SX, SY, None, SB)
             high[SA], low[SA] = high[SR], low[SR]
 
         @pl.when(swap_y & (chip == 1))
         def _():
             for i in range(2):
-                multiply(i, SC, SY, None, SA)
+                multiply(i * half, (i + 1) * half, SC, SY, None, SA)
             high[SB], low[SB] = high[SY], low[SY]
 
         @pl.when(swap_y & (chip == 2))
@@ -493,7 +495,7 @@
         @pl.when(hand)
         def _():
             for i in range(2):
-                multiply(i, SM, SB, LAST)
+                multiply(i * half, (i + 1) * half, SM, SB, LAST)
 
         send_factor(hand, LAST, LAST, core, E_LAST)
 
@@ -698,15 +700,18 @@
     def _():
         high[SA], low[SA] = high[SM], low[SM]
 
-    for part, recv in ((0, R_FACTOR[ZF]), (2, R_ENDS)):
+    for parts, ref, recv in (
+        ((0, 1, 2, 3), pm.at[ZF, :half, :WIDE], R_FACTOR[ZF]), ((4, 5), factor(ZF)[4], R_ENDS),
+    ):
         @pl.when(bottom & even)
-        def _(part=part, recv=recv):
-            ref = factor(ZF)[part]
+        def _(ref=ref, recv=recv):
             copy(ref, ref, sent.at[0], got.at[recv], me).wait_recv()
 
+        count = len(parts) // 2
         for i in range(2):
-            send_factor(bottom & even & (b1 == i), ZF, ZF, px, E_X, (part + i,), recv=R_ZF2, last=None)
-            send_factor(bottom & even & (b1 == i), ZF, YF, core, E_ALL, (part + i,), last=None)
+            mine = parts[i * count:(i + 1) * count]
+            send_factor(bottom & even & (b1 == i), ZF, ZF, px, E_X, mine, recv=R_ZF2, last=None)
+            send_factor(bottom & even & (b1 == i), ZF, YF, core, E_ALL, mine, last=None)
 
     @pl.when(even)
     def _():
@@ -718,7 +723,7 @@
         copy(half_tally, half_tally, sent.at[0], got.at[R_ZF2], me).wait_recv()
 
     for i in range(2):
-        send_factor(bottom & even & (b1 != i), ZF, YF, core, E_ALL, (i, 2 + i), last=None)
+        send_factor(bottom & even & (b1 != i), ZF, YF, core, E_ALL, (2 * i, 2 * i + 1, 4 + i), last=None)
 
     @pl.when(bottom & even)
     def _():

time: 37.6 us -> 37.5 us (level)
  no operation moved by 1% of the time
where the time goes in v7:
time: 37.5 us; the launch traced here: 37.3 us
  Pallas kernels  36.5 us (97%)
  between operations  0.8 us (2%)
    pallas_call x1, Pallas kernels, local(): pl.pallas_call(functools.partial(kernel, n), out_shape=[pltpu.VMEM(full,...  35.1 us
    pallas_call x1, Pallas kernels, local(): pl.pallas_call(finish, out_shape=[jax.ShapeDtypeStruct(full, f32)] * 2, i...  1.42 us

profile of v7, /device:TPU:0, one launch (start us, length us, event | category | flops | bytes accessed | tf_op | source)
XLA Modules:
  0.0 37.3 jit_solution(8611131270046108968)
XLA Ops:
  0.6 35.1 %shard_map.41 = (f32[320,320]{1,0:T(8,128)S(1)}, bf16[320,320]{1,0:T(8,128)(2,1)S(1)}, bf16[320,320]{1,0:T(8,128)(2,1)S(1)}, bf16[320,320]{1,0:T(8,128)(2,1)S(1)}, bf16[320,320]{1,0:T(8,128)(2,1)S(1)}) custom-call(f32[320,320]{1,0:T(8,128)} %bitcast.4, f32[320,320]{1,0:T(8,128)} %bitcast.5), custom_call_target="tpu_custom_call" | custom-call | tf_op jit(solution)/shard_map/pallas_call | solution.py:823
  35.7 1.4 %shard_map.42 = (f32[320,320]{1,0:T(8,128)}, f32[320,320]{1,0:T(8,128)}) custom-call(f32[320,320]{1,0:T(8,128)S(1)} %get-tuple-element.9.x_ref, bf16[320,320]{1,0:T(8,128)(2,1)S(1)} %get-tuple-element.10.xh, bf16[320,320]{1,0:T(8,128)(2,1)S(1)} %get-tuple-element.11.xl, bf16[320,320]{1,0:T(8,128)(2,1)S(1)} %get-tuple-element.12.qh, ...), custom_call_target="tpu_custom_call" | custom-call | tf_op jit(solution)/shard_map/pallas_call | solution.py:841

commit v8 on v7

--- a/solution.py
+++ b/solution.py
@@ -464,11 +464,12 @@
             @pl.when(even & hears)
             def _(i=i):
                 multiply(i * half, (i + 1) * half, SA, SB, ALL, SR)
+            send_factor(even_chain, ALL, ALL, core, E_ALL, (2 * i, 2 * i + 1))
             send_factor(down & (b1 == i), ALL, ZF, me - GROUP, E_ALL, (2 * i, 2 * i + 1))
         for i in range(2):
             send_factor(down & (b1 == i), ALL, ZF, me - GROUP, E_ALL, (4 + i,), recv=R_ENDS, last=None)
         leave(down, lambda: half_tally, E_ALL)
-        send_factor(even_chain, ALL, ALL, core, E_ALL)
+        send_factor(even_chain, ALL, ALL, core, E_ALL, (4, 5))
 
         @pl.when(swap_y & (chip == 0))
         def _():

time: 37.5 us -> 37.5 us (level)
  no operation moved by 1% of the time
where the time goes in v8:
time: 37.5 us; the launch traced here: 37.3 us
  Pallas kernels  36.5 us (97%)
  between operations  0.8 us (2%)
    pallas_call x1, Pallas kernels, local(): pl.pallas_call(functools.partial(kernel, n), out_shape=[pltpu.VMEM(full,...  35.1 us
    pallas_call x1, Pallas kernels, local(): pl.pallas_call(finish, out_shape=[jax.ShapeDtypeStruct(full, f32)] * 2, i...  1.42 us

profile of v8, /device:TPU:0, one launch (start us, length us, event | category | flops | bytes accessed | tf_op | source)
XLA Modules:
  0.0 37.3 jit_solution(17115444839421736964)
XLA Ops:
  0.6 35.1 %shard_map.41 = (f32[320,320]{1,0:T(8,128)S(1)}, bf16[320,320]{1,0:T(8,128)(2,1)S(1)}, bf16[320,320]{1,0:T(8,128)(2,1)S(1)}, bf16[320,320]{1,0:T(8,128)(2,1)S(1)}, bf16[320,320]{1,0:T(8,128)(2,1)S(1)}) custom-call(f32[320,320]{1,0:T(8,128)} %bitcast.4, f32[320,320]{1,0:T(8,128)} %bitcast.5), custom_call_target="tpu_custom_call" | custom-call | tf_op jit(solution)/shard_map/pallas_call | solution.py:824
  35.7 1.4 %shard_map.42 = (f32[320,320]{1,0:T(8,128)}, f32[320,320]{1,0:T(8,128)}) custom-call(f32[320,320]{1,0:T(8,128)S(1)} %get-tuple-element.9.x_ref, bf16[320,320]{1,0:T(8,128)(2,1)S(1)} %get-tuple-element.10.xh, bf16[320,320]{1,0:T(8,128)(2,1)S(1)} %get-tuple-element.11.xl, bf16[320,320]{1,0:T(8,128)(2,1)S(1)} %get-tuple-element.12.qh, ...), custom_call_target="tpu_custom_call" | custom-call | tf_op jit(solution)/shard_map/pallas_call | solution.py:842
